TPU v7x, 32 devices: a whole 2x2x4 slice. The times are simulated.
32 devices in a mesh: sta: 16 (over z, y, core), band: 2 (over x).
Axes of the slice: x: 2, y: 2, z: 4, core: 2. Of those that a mesh axis runs over, the one named last changes fastest.
Arguments:
- traces: bfloat16 [64, 8, 16384], P('sta', 'band'), may hold values from -400 to 400, as said below
- live_flag: int32 [64, 8], P('sta'), may hold values 0 or 1
- response: float32 [8192], P('band'), may hold values from 0.3 to 3
Outputs:
- own_cross: bfloat16 [2, 64, 4, 8192], P(None, 'sta', None, 'band')
- near_cross: bfloat16 [2, 64, 4, 8192], P(None, 'sta', None, 'band')
- far_cross: bfloat16 [2, 64, 4, 8192], P(None, 'sta', None, 'band')
Inputs may be any that keep to these rules, and one draw needn't show every extreme that they name: `traces`: recorded ground motion of each station and window.
All inputs are finite; a program needn't handle non-finite values. No bound on the sum of `live_flag` on one device may be relied on, other than what follows from the above.
Results may differ from a plain program's by a relative error of at most 0.008.
Values may be sent and summed in bfloat16 or wider, within the bound.
No kernel may reach another device: no remote copies, remote signals or barrier semaphores. Data moves between devices by JAX's collectives and lax.ppermute only.
A program may use at most 64 MiB of HBM per device.

v0:
```python
import functools
import math

import jax
import jax.numpy as jnp
import numpy as np
from jax import lax
from jax.experimental import pallas as pl
from jax.experimental.pallas import tpu as pltpu
from jax.sharding import PartitionSpec as P


ROOT = 128
SMOOTH = 64
epsilon = 1e-06

C_HALVES = True
X_HALVES = True
O_HALVES = True
DIAGONAL = ()
DIRECT = ("1_1",)


@functools.cache
def tables():
    n = np.arange(ROOT)
    angle = 2.0 * math.pi * ((n[:, None] * n[None, :]) % ROOT) / ROOT
    first = np.concatenate([np.cos(angle), -np.sin(angle)], axis=1)
    step = 2.0 * math.pi * n[None, :] / (ROOT * ROOT)
    coarse, fine = 8 * np.arange(ROOT // 8)[:, None] * step, np.arange(8)[:, None] * step
    turns = [np.cos(coarse), np.sin(coarse), np.cos(fine), np.sin(fine)]
    return (
        jnp.asarray(first.T, jnp.bfloat16),
        jnp.asarray(np.concatenate(turns, axis=0), jnp.float32),
    )


@functools.cache
def smoother():
    src = np.arange(3 * ROOT)[:, None] - ROOT
    dst = np.arange(ROOT)[None, :]
    return jnp.asarray(np.abs(src - dst) <= SMOOTH, jnp.bfloat16)


def parts_of(stations):
    return 2 if stations % 2 == 0 else 1


def transformed(x, gate, held, outs, wide, edges, stations, windows, bands):
    first, cosine, sine = held
    half = ROOT // 2
    rows = half // bands
    cos_part, sin_part = first[:half, :], first[ROOT : ROOT + half, :]
    second = jnp.concatenate(
        [
            jnp.concatenate([cos_part, -sin_part], axis=1),
            jnp.concatenate([sin_part, cos_part], axis=1),
        ],
        axis=0,
    )
    lane = lax.broadcasted_iota(jnp.int32, (1, ROOT), 1)
    none = jnp.zeros((1, ROOT), jnp.float32)
    for s in range(stations):
        wide[...] = x(s).astype(jnp.float32)
        folded = jnp.concatenate(
            [
                wide[pl.ds(w, ROOT, stride=windows), :].astype(jnp.bfloat16)
                for w in range(windows)
            ],
            axis=1,
        )
        one = jnp.dot(first[...], folded, preferred_element_type=jnp.float32)
        for w in range(windows):
            real = one[:ROOT, w * ROOT : (w + 1) * ROOT]
            imag = one[ROOT:, w * ROOT : (w + 1) * ROOT]
            turned = jnp.concatenate(
                [
                    real * cosine[...] + imag * sine[...],
                    imag * cosine[...] - real * sine[...],
                ],
                axis=1,
            ).astype(jnp.bfloat16)
            at = s * windows + w
            two = lax.dot_general(
                second, turned, (((1,), (1,)), ((), ())),
                preferred_element_type=jnp.float32,
            ) * gate(at)
            for k in range(bands):
                low, high = k * rows, (k + 1) * rows
                for e in range(2):
                    part = two[e * half : (e + 1) * half]
                    after = part[high : high + 1] if high < half else none
                    before = part[low - 1 : low] if low else none
                    edges[k, pl.ds(2 * at + e, 1), :] = jnp.where(lane < SMOOTH, after, before)
                both = jnp.concatenate([two[low:high], two[half + low : half + high]], axis=0)
                outs[k][pl.ds(2 * at * rows, 2 * rows), :] = both.astype(jnp.bfloat16)
    lines = 2 * stations * windows
    for k in range(bands):
        outs[k][pl.ds(lines * rows, lines), :] = edges[k].astype(jnp.bfloat16)


def first_half_kernel(given_flags, x_ref, given, given_turns, *refs, stations, windows, bands):
    parts = parts_of(stations)
    per = stations // parts
    outs, held, refs = refs[:bands], refs[bands : bands + 3], refs[bands + 3 :]
    if parts > 1:
        later, gates, *refs = refs
    now, turns, wide, edges, flag_ref, sems = refs
    here = lax.axis_index("band").astype(jnp.int32)
    load_flags = pltpu.make_async_copy(given_flags, flag_ref, sems.at[3 + per])
    load_turns = pltpu.make_async_copy(given_turns, turns, sems.at[0])
    load_first = pltpu.make_async_copy(given, held[0], sems.at[1])
    arrivals = [
        pltpu.make_async_copy(x_ref.at[s], now.at[s], sems.at[2 + s]) for s in range(per)
    ]
    for load in (load_flags, load_turns, load_first, *arrivals):
        load.start()
    if parts > 1:
        rest = pltpu.make_async_copy(x_ref.at[pl.ds(per, per)], later, sems.at[2 + per])
        rest.start()

    def flag(at):
        return flag_ref[at // windows, here * windows + at % windows].astype(jnp.float32)

    load_flags.wait()
    if parts > 1:
        for at in range(per * windows):
            gates[pl.ds(at, 1), :] = jnp.full((1, ROOT), flag(per * windows + at), jnp.float32)
    load_turns.wait()
    count = ROOT // 8
    fine_cos, fine_sin = turns[2 * count : 2 * count + 8, :], turns[2 * count + 8 :, :]
    for i in range(count):
        cos, sin = turns[i : i + 1, :], turns[count + i : count + i + 1, :]
        held[1][pl.ds(8 * i, 8), :] = cos * fine_cos - sin * fine_sin
        held[2][pl.ds(8 * i, 8), :] = sin * fine_cos + cos * fine_sin
    load_first.wait()

    def x(s):
        arrivals[s].wait()
        return now[s]

    transformed(x, flag, held, outs, wide, edges, per, windows, bands)
    if parts > 1:
        rest.wait()


def second_half_kernel(x_ref, gates, *refs, stations, windows, bands):
    held, outs, (wide, edges) = refs[:3], refs[3 : 3 + bands], refs[3 + bands :]
    transformed(
        lambda s: x_ref[s], lambda at: gates[pl.ds(at, 1), :], held, outs, wide, edges,
        stations, windows, bands,
    )


def transform(traces, live_flag, bands):
    stations, windows, _ = traces.shape
    packed = traces.reshape(stations, windows, ROOT, ROOT).transpose(0, 2, 1, 3)
    packed = packed.reshape(stations, ROOT * windows, ROOT)
    rows = ROOT // 2 // bands
    parts = parts_of(stations)
    per = stations // parts
    height = 2 * per * windows * (rows + 1)
    vmem = pl.BlockSpec(memory_space=pltpu.VMEM)
    hbm = pl.BlockSpec(memory_space=pl.ANY)
    piece = pltpu.VMEM((height, ROOT), jnp.bfloat16)
    given = tables()
    shape = (per, ROOT * windows, ROOT)
    turned = pltpu.VMEM((ROOT, ROOT), jnp.float32)
    outs = [piece] * bands + [pltpu.VMEM(given[0].shape, jnp.bfloat16), turned, turned]
    if parts > 1:
        outs += [pltpu.VMEM(shape, jnp.bfloat16), pltpu.VMEM((per * windows, ROOT), jnp.float32)]
    scratch = [
        pltpu.VMEM((ROOT * windows, ROOT), jnp.float32),
        pltpu.VMEM((bands, 2 * per * windows, ROOT), jnp.float32),
    ]
    made = pl.pallas_call(
        functools.partial(first_half_kernel, stations=stations, windows=windows, bands=bands),
        out_shape=outs,
        in_specs=[hbm] * 4,
        out_specs=[vmem] * len(outs),
        scratch_shapes=[
            pltpu.VMEM(shape, jnp.bfloat16), pltpu.VMEM(given[1].shape, jnp.float32), *scratch,
            pltpu.SMEM(live_flag.shape, jnp.int32), pltpu.SemaphoreType.DMA((4 + per,)),
        ],
        name="transform_first",
    )(live_flag, packed, *given)
    halves = [made[:bands]]
    if parts > 1:
        held, later, gates = made[bands : bands + 3], made[bands + 3], made[bands + 4]
        args = [pltpu.with_memory_space_constraint(v, pltpu.VMEM) for v in (later, gates, *held)]
        halves.append(
            pl.pallas_call(
                functools.partial(second_half_kernel, stations=per, windows=windows, bands=bands),
                out_shape=[piece] * bands,
                in_specs=[vmem] * len(args),
                out_specs=[vmem] * bands,
                scratch_shapes=scratch,
                name="transform_second",
            )(*args)
        )
    return [[half[k] for half in halves] for k in range(bands)]


def scales_of(power, edge, gain, window, stations, rows, total):
    spread = []
    for s in range(stations):
        own = power[s * rows : (s + 1) * rows]
        beside = edge[s : s + 1]
        before = jnp.concatenate([beside, own[:-1]], axis=0)
        after = jnp.concatenate([own[1:], beside], axis=0)
        spread.append(jnp.concatenate([before, own, after], axis=1))
    spread = jnp.concatenate(spread, axis=0)
    high = spread.astype(jnp.bfloat16)
    low = (spread - high.astype(jnp.float32)).astype(jnp.bfloat16)
    smooth = jnp.dot(low, window, preferred_element_type=jnp.float32)
    smooth = smooth + jnp.dot(high, window, preferred_element_type=jnp.float32)
    smooth = smooth * (1.0 / ((2 * SMOOTH + 1) * total))
    return jnp.concatenate([gain] * stations, axis=0) / jnp.sqrt(smooth + epsilon)


def cross_kernel(*refs, stations, windows, rows, merges, theirs, total, own, first, last):
    refs = list(refs)
    chunks, parts = len(merges), parts_of(stations)
    per = stations // parts

    def take(count):
        taken, refs[:] = refs[:count], refs[count:]
        return taken

    def views(flags):
        pieces = []
        for merged in flags:
            if merged:
                height = 2 * per * windows * (rows + 1)
                (ref,) = take(1)
                pieces += [(ref, h * height) for h in range(parts)]
            else:
                pieces += [(ref, 0) for ref in take(parts)]
        return pieces

    left = views(merges)
    right = left if own else views(theirs)
    if not first:
        sums, power_in, edge_in = take(3)
    if last:
        gain, window = take(2)
        scale_left = None if own else take(1)[0]
        (out,) = take(1)
        scale_right, board, ready, sems = take(4)
        scale_left = scale_right if own else scale_left
    else:
        sums_out, power_out, edge_out = take(3)

    body = 2 * per * windows * rows
    power, edge = [], []
    for s in range(stations):
        cells = []
        lines = []
        for k in range(chunks):
            chunk, base = right[k * parts + s // per]
            for w in range(windows):
                at = 2 * (s % per * windows + w)
                cell = chunk[pl.ds(base + at * rows, 2 * rows), :].astype(jnp.float32)
                cell = cell * cell
                cells.append(cell[:rows] + cell[rows:])
            line = chunk[pl.ds(base + body + 2 * (s % per) * windows, 2 * windows), :]
            line = line.astype(jnp.float32)
            lines.append(jnp.sum(line * line, axis=0, keepdims=True))
        power.append(sum(cells[1:], cells[0]))
        edge.append(sum(lines[1:], lines[0]))
    power, edge = jnp.concatenate(power, axis=0), jnp.concatenate(edge, axis=0)
    if not first:
        power, edge = power + power_in[...], edge + edge_in[...]
    if last:
        scale_right[...] = scales_of(power, edge, gain[...], window[...], stations, rows, total)
    else:
        power_out[...], edge_out[...] = power, edge

    step = min(16, rows)
    steps = rows // step

    def stored(e, i):
        return pltpu.make_async_copy(ready.at[e, i], out.at[e, i], sems.at[e, i])

    def tree(terms):
        while len(terms) > 1:
            terms = [x + y for x, y in zip(terms[::2], terms[1::2])] + (
                terms[-1:] if len(terms) % 2 else []
            )
        return terms[0].astype(jnp.float32)

    for i in range(stations):

        def turn(index, carry, i=i):
            q = pl.multiple_of(index * step, step)
            real, imag = [None] * stations, [None] * stations

            def cell(pieces, k, s, w, e):
                ref, base = pieces[k * parts + s // per]
                at = base + ((s % per * windows + w) * 2 + e) * rows
                return ref[pl.ds(pl.multiple_of(at + q, step), step), :]

            for k in range(chunks):
                a = [cell(left, k, i, w, 0) for w in range(windows)]
                b = [cell(left, k, i, w, 1) for w in range(windows)]
                for j in range(stations):
                    c = [cell(right, k, j, w, 0) for w in range(windows)]
                    d = [cell(right, k, j, w, 1) for w in range(windows)]
                    re = tree([a[w] * c[w] + b[w] * d[w] for w in range(windows)])
                    im = tree([b[w] * c[w] - a[w] * d[w] for w in range(windows)])
                    real[j] = re if k == 0 else real[j] + re
                    imag[j] = im if k == 0 else imag[j] + im
            if last:
                here = scale_left[pl.ds(pl.multiple_of(i * rows + q, step), step), :]
                here = here * (1.0 / total)
            for j in range(stations):
                to = pl.ds(q, step)
                if not first:
                    real[j] = real[j] + sums[0, i, j, to, :]
                    imag[j] = imag[j] + sums[1, i, j, to, :]
                if last:
                    there = scale_right[pl.ds(pl.multiple_of(j * rows + q, step), step), :]
                    to = pl.ds(q * stations + j, step, stride=stations)
                    board[0, to, :] = real[j] * (here * there)
                    board[1, to, :] = imag[j] * (here * there)
                else:
                    sums_out[0, i, j, to, :] = real[j]
                    sums_out[1, i, j, to, :] = imag[j]
            return carry

        lax.fori_loop(0, steps, turn, 0)
        if last:
            ready[:, i] = board[...].astype(jnp.bfloat16)
            for e in range(2):
                stored(e, i).start()
    if last:
        for i in range(stations):
            for e in range(2):
                stored(e, i).wait()


def cross(left, right, stations, windows, total, before=None, ends=None):
    own = right is None
    first, last = before is None, ends is not None
    merges, theirs = (
        tuple(len(chunk) == 1 and parts_of(stations) > 1 for chunk in side)
        for side in (left, right or left)
    )
    height = sum(piece.shape[0] for piece in left[0])
    rows = height // (2 * stations * windows) - 1
    vmem = pl.BlockSpec(memory_space=pltpu.VMEM)
    shape = (2, stations, rows * stations, ROOT)
    scales = (stations * rows, ROOT)
    args = [piece for chunk in (*left, *(right or ())) for piece in chunk]
    args += [*(before or ()), *(ends or ())]
    args = [pltpu.with_memory_space_constraint(c, pltpu.VMEM) for c in args]
    if last:
        outs = [jax.ShapeDtypeStruct(shape, jnp.bfloat16)]
        out_specs = [pl.BlockSpec(memory_space=pl.ANY)]
        scratch = [
            pltpu.VMEM((2, *shape[2:]), jnp.float32),
            pltpu.VMEM(shape, jnp.bfloat16),
            pltpu.SemaphoreType.DMA((2, stations)),
        ]
        if own:
            outs.append(pltpu.VMEM(scales, jnp.float32))
            out_specs.append(vmem)
        else:
            scratch.insert(0, pltpu.VMEM(scales, jnp.float32))
    else:
        outs = [
            pltpu.VMEM((2, stations, stations, rows, ROOT), jnp.float32),
            pltpu.VMEM(scales, jnp.float32),
            pltpu.VMEM((stations, ROOT), jnp.float32),
        ]
        out_specs = [vmem] * 3
        scratch = []
    result = pl.pallas_call(
        functools.partial(
            cross_kernel, stations=stations, windows=windows, rows=rows, merges=merges,
            theirs=theirs,            total=total, own=own, first=first, last=last,
        ),
        out_shape=outs,
        in_specs=[vmem] * len(args),
        out_specs=out_specs,
        scratch_shapes=scratch,
        name="own_cross" if own else "pair_cross" if last else "pair_sums",
    )(*args)
    if not last:
        return result
    spread = result[0].reshape(2, stations, rows, stations, ROOT).transpose(0, 1, 3, 2, 4)
    spread = spread.reshape(2, stations, stations, rows * ROOT)
    return (spread, result[1]) if own else spread


def brought(block, axis, distance):
    count = lax.axis_size(axis)
    return lax.ppermute(block, axis, [((i + distance) % count, i) for i in range(count)])


def program(traces, live_flag, response):
    stations, windows, _ = traces.shape
    bands, parts = lax.axis_size("band"), parts_of(stations)
    band = lax.axis_index("band").astype(jnp.int32)
    blocks = lax.axis_size("sta")
    offset = blocks // 8
    total = live_flag.shape[1]
    split = transform(traces, live_flag, bands)
    even = lax.rem(lax.div(lax.axis_index("sta"), offset), 2) == 0
    relay = [(i, i + offset if i // offset % 2 == 0 else i - offset) for i in range(blocks)]

    def sent(k, h):
        pieces = [split[b][h] for b in range(bands)]
        if bands == 2:
            return jnp.where(band == k, *pieces)
        return lax.select_n((band + k) % bands, *pieces) if bands > 1 else pieces[0]

    def joined(k, hs):
        return jnp.concatenate([sent(k, h) for h in hs], axis=0) if hs[1:] else sent(k, hs[0])

    def groups(halves):
        return [(h,) for h in range(parts)] if halves else [tuple(range(parts))]

    def across(piece, distance, k):
        if not k:
            return brought(piece, "sta", distance)
        route = [
            ((s + distance) % blocks * bands + (b - k) % bands, s * bands + b)
            for s in range(blocks)
            for b in range(bands)
        ]
        return lax.ppermute(piece, ("sta", "band"), route)

    mine, far, near = ([[] for _ in range(bands)] for _ in range(3))
    for k in range(bands):
        for hs in groups(X_HALVES if k else C_HALVES):
            piece = joined(k, hs)
            mine[k].append(brought(piece, "band", -k) if k else piece)
    for k in range(bands):
        for at, hs in enumerate(groups(O_HALVES if k else C_HALVES)):
            tag = f"{min(k, 1)}_{hs[0]}"
            if k and tag not in DIAGONAL:
                piece = mine[k][at]
                far[k].append(brought(piece, "sta", 2 * offset))
            else:
                piece = joined(k, hs)
                far[k].append(across(piece, 2 * offset, k))
            if tag in DIRECT:
                near[k].append(across(joined(k, hs), offset, k) if tag in DIAGONAL else brought(piece, "sta", offset))
            else:
                held = mine[k]
                if len(held) > 1 or not O_HALVES or not k:
                    held = held[at]
                else:
                    size = held[0].shape[0] // parts
                    held = held[0][at * size : (at + 1) * size]
                near[k].append(lax.ppermute(jnp.where(even, far[k][-1], held), "sta", relay))
    ends = [response.reshape(-1, ROOT), smoother()]
    own_cross, scale = cross(mine, None, stations, windows, total, ends=ends)
    ends.append(scale)

    def pair(theirs):
        if bands == 1:
            return cross(mine, theirs, stations, windows, total, ends=ends)
        sums = cross(mine[:1], theirs[:1], stations, windows, total)
        return cross(mine[1:], theirs[1:], stations, windows, total, before=sums, ends=ends)

    far_cross = pair(far)
    near_cross = pair(near)
    return own_cross, near_cross, far_cross


def solution(mesh):
    in_specs = (P("sta", "band", None), P("sta", None), P("band"))
    out_specs = (P(None, "sta", None, "band"),) * 3
    return jax.shard_map(program, mesh=mesh, in_specs=in_specs, out_specs=out_specs, check_vma=False)
```

profile of v0, /device:TPU:0, one launch (start us, length us, event | category | flops | bytes accessed | tf_op | source)
XLA Modules:
  0.0 29.8 jit_solution(1440176233193674711)
XLA Ops:
  0.6 1.9 %transform_first.1 = (bf16[528,128]{1,0:T(8,128)(2,1)S(1)}, bf16[528,128]{1,0:T(8,128)(2,1)S(1)}, bf16[256,128]{1,0:T(8,128)(2,1)S(1)}, f32[128,128]{1,0:T(8,128...) custom-call(s32[4,8]{1,0:T(4,128)} %given_flags.1, ...), custom_call_target="tpu_custom_call" | custom-call | tf_op jit(solution)/shard_map/transform_first/pallas_call | solution.py:176
  2.5 0.7 %transform_second.1 = (bf16[528,128]{1,0:T(8,128)(2,1)S(1)}, bf16[528,128]{1,0:T(8,128)(2,1)S(1)}) custom-call(bf16[2,512,128]{2,1,0:T(8,128)(2,1)S(1)} %get-tuple-element.22.x_ref, f32[8,128]{1,0:T(8,128)S(1)} %get-tuple-element.23.gates, bf16[256,128]{1,0:T(8,128)(2,1)S(1)} %get-tuple-element.24.refs_0_, f32[128,128]{1,0:T(8,128)S(1)} %get-tuple-element.25.refs_1_, ...), custom_call_target="tpu_custom_call" | custom-call | tf_op jit(solution)/shard_map/transform_second/pallas_call | solution.py:192
  3.3 5.1 %collective-permute-start.7 = (bf16[528,128]{1,0:T(8,128)(2,1)S(1)}, bf16[528,128]{1,0:T(8,128)(2,1)S(1)}, u32[]{:S(2)}, u32[]{:S(2)}) collective-permute-start(bf16[528,128]{1,0:T(8,128)(2,1)S(1)} %get-tuple-element.38.refs_1_), channel_id=1, source_target_pairs={{8,0},{10,2},{12,4},{14,6},{16,8},{18,10},{20,12},{22,14},{24,16},... | collective-permute-start | bytes 405512 | tf_op jit(solution)/shard_map/ppermute | solution.py:398
  8.5 0.5 %collective-permute-start.5 = (bf16[528,128]{1,0:T(8,128)(2,1)S(1)}, bf16[528,128]{1,0:T(8,128)(2,1)S(1)}, u32[]{:S(2)}, u32[]{:S(2)}) collective-permute-start(bf16[528,128]{1,0:T(8,128)(2,1)S(1)} %get-tuple-element.40.refs_0_), channel_id=1, source_target_pairs={{8,0},{10,2},{12,4},{14,6},{16,8},{18,10},{20,12},{22,14},{24,16},... | collective-permute-start | bytes 405512 | tf_op jit(solution)/shard_map/ppermute | solution.py:398
  9.0 1.5 %collective-permute-start.1 = (bf16[528,128]{1,0:T(8,128)(2,1)S(1)}, bf16[528,128]{1,0:T(8,128)(2,1)S(1)}, u32[]{:S(2)}, u32[]{:S(2)}) collective-permute-start(bf16[528,128]{1,0:T(8,128)(2,1)S(1)} %get-tuple-element.37), channel_id=1, source_target_pairs={{1,0},{0,1},{3,2},{2,3},{5,4},{4,5},{7,6},{6,7},{9,8},{8,9},{11,10... | collective-permute-start | bytes 405512 | tf_op jit(solution)/shard_map/ppermute | solution.py:398
  10.4 0.5 %collective-permute-start = (bf16[528,128]{1,0:T(8,128)(2,1)S(1)}, bf16[528,128]{1,0:T(8,128)(2,1)S(1)}, u32[]{:S(2)}, u32[]{:S(2)}) collective-permute-start(bf16[528,128]{1,0:T(8,128)(2,1)S(1)} %get-tuple-element.39), channel_id=1, source_target_pairs={{1,0},{0,1},{3,2},{2,3},{5,4},{4,5},{7,6},{6,7},{9,8},{8,9},{11,10... | collective-permute-start | bytes 405512 | tf_op jit(solution)/shard_map/ppermute | solution.py:398
  11.0 1.4 %collective-permute-done.7.refs_3_ = bf16[528,128]{1,0:T(8,128)(2,1)S(1)} collective-permute-done((bf16[528,128]{1,0:T(8,128)(2,1)S(1)}, bf16[528,128]{1,0:T(8,128)(2,1)S(1)}, u32[]{:S(2)}, u32[]{:S(2)}) %collective-permute-start.7) | collective-permute-done | bytes 135200 | tf_op jit(solution)/shard_map/ppermute | solution.py:398
  12.4 1.6 %collective-permute-start.8 = (bf16[528,128]{1,0:T(8,128)(2,1)S(1)}, bf16[528,128]{1,0:T(8,128)(2,1)S(1)}, u32[]{:S(2)}, u32[]{:S(2)}) collective-permute-start(bf16[528,128]{1,0:T(8,128)(2,1)S(1)} %broadcast_select_fusion), channel_id=1, source_target_pairs={{0,4},{2,6},{4,0},{6,2},{8,12},{10,14},{12,8},{14,10},{16,20},{18,... | collective-permute-start | bytes 405512 | tf_op jit(solution)/shard_map/ppermute | solution.py:457
  14.0 2.6 %collective-permute-done.refs_2_.refs_0_ = bf16[528,128]{1,0:T(8,128)(2,1)S(1)} collective-permute-done((bf16[528,128]{1,0:T(8,128)(2,1)S(1)}, bf16[528,128]{1,0:T(8,128)(2,1)S(1)}, u32[]{:S(2)}, u32[]{:S(2)}) %collective-permute-start) | collective-permute-done | bytes 135200 | tf_op jit(solution)/shard_map/ppermute | solution.py:398
  16.6 1.7 %collective-permute-start.2 = (bf16[528,128]{1,0:T(8,128)(2,1)S(1)}, bf16[528,128]{1,0:T(8,128)(2,1)S(1)}, u32[]{:S(2)}, u32[]{:S(2)}) collective-permute-start(bf16[528,128]{1,0:T(8,128)(2,1)S(1)} %collective-permute-done.refs_2_.refs_0_), channel_id=1, source_target_pairs={{8,0},{10,2},{12,4},{14,6},{16,8},{18,10},{20,12},{22,14},{24,16},... | collective-permute-start | bytes 405512 | tf_op jit(solution)/shard_map/ppermute | solution.py:398
  18.3 0.0 collective-permute-done.5.refs_2_
  18.3 0.6 %collective-permute-start.6 = (bf16[528,128]{1,0:T(8,128)(2,1)S(1)}, bf16[528,128]{1,0:T(8,128)(2,1)S(1)}, u32[]{:S(2)}, u32[]{:S(2)}) collective-permute-start(bf16[528,128]{1,0:T(8,128)(2,1)S(1)} %broadcast_select_fusion.1), channel_id=1, source_target_pairs={{0,4},{2,6},{4,0},{6,2},{8,12},{10,14},{12,8},{14,10},{16,20},{18,... | collective-permute-start | bytes 405512 | tf_op jit(solution)/shard_map/ppermute | solution.py:457
  18.9 0.0 collective-permute-done.1.refs_3_.refs_1_
  18.9 1.2 %collective-permute-start.9 = (bf16[528,128]{1,0:T(8,128)(2,1)S(1)}, bf16[528,128]{1,0:T(8,128)(2,1)S(1)}, u32[]{:S(2)}, u32[]{:S(2)}) collective-permute-start(bf16[528,128]{1,0:T(8,128)(2,1)S(1)} %collective-permute-done.1.refs_3_.refs_1_), channel_id=1, source_target_pairs={{8,0},{10,2},{12,4},{14,6},{16,8},{18,10},{20,12},{22,14},{24,16},... | collective-permute-start | bytes 405512 | tf_op jit(solution)/shard_map/ppermute | solution.py:398
  20.1 2.6 %collective-permute-start.4 = (bf16[528,128]{1,0:T(8,128)(2,1)S(1)}, bf16[528,128]{1,0:T(8,128)(2,1)S(1)}, u32[]{:S(2)}, u32[]{:S(2)}) collective-permute-start(bf16[528,128]{1,0:T(8,128)(2,1)S(1)} %collective-permute-done.1.refs_3_.refs_1_), channel_id=1, source_target_pairs={{4,0},{6,2},{8,4},{10,6},{12,8},{14,10},{16,12},{18,14},{20,16},{2... | collective-permute-start | bytes 405512 | tf_op jit(solution)/shard_map/ppermute | solution.py:398
  22.7 0.4 %collective-permute-done.2.refs_2_ = bf16[528,128]{1,0:T(8,128)(2,1)S(1)} collective-permute-done((bf16[528,128]{1,0:T(8,128)(2,1)S(1)}, bf16[528,128]{1,0:T(8,128)(2,1)S(1)}, u32[]{:S(2)}, u32[]{:S(2)}) %collective-permute-start.2) | collective-permute-done | bytes 135200 | tf_op jit(solution)/shard_map/ppermute | solution.py:398
  23.1 0.0 copy-start
  23.1 0.0 copy-start.1
  23.1 0.5 %collective-permute-start.3 = (bf16[528,128]{1,0:T(8,128)(2,1)S(1)}, bf16[528,128]{1,0:T(8,128)(2,1)S(1)}, u32[]{:S(2)}, u32[]{:S(2)}) collective-permute-start(bf16[528,128]{1,0:T(8,128)(2,1)S(1)} %broadcast_select_fusion.2), channel_id=1, source_target_pairs={{0,4},{2,6},{4,0},{6,2},{8,12},{10,14},{12,8},{14,10},{16,20},{18,... | collective-permute-start | bytes 405512 | tf_op jit(solution)/shard_map/ppermute | solution.py:457
  23.6 0.5 %pair_sums.3 = (f32[2,4,4,32,128]{4,3,2,1,0:T(8,128)S(1)}, f32[128,128]{1,0:T(8,128)S(1)}, f32[4,128]{1,0:T(4,128)S(1)}) custom-call(bf16[528,128]{1,0:T(8,128)(2,1)S(1)} %get-tuple-element.40.refs_0_, bf16[528,128]{1,0:T(8,128)(2,1)S(1)} %get-tuple-element.38.refs_1_, bf16[528,128]{1,0:T(8,128)(2,1)S(1)} %collective-permute-done.5.refs_2_, ...), custom_call_target="tpu_custom_call" | custom-call | tf_op jit(solution)/shard_map/pair_sums/pallas_call | solution.py:378
  24.1 0.0 copy-done
  24.1 0.0 copy-done.1
  24.1 1.9 %own_cross.1 = (bf16[2,4,128,128]{3,2,1,0:T(8,128)(2,1)}, f32[128,128]{1,0:T(8,128)S(1)}) custom-call(bf16[528,128]{1,0:T(8,128)(2,1)S(1)} %get-tuple-element.40.refs_0_, bf16[528,128]{1,0:T(8,128)(2,1)S(1)} %get-tuple-element.38.refs_1_, bf16[528,128]{1,0:T(8,128)(2,1)S(1)} %collective-permute-done.refs_2_.refs_0_, ...), custom_call_target="tpu_custom_call" | custom-call | tf_op jit(solution)/shard_map/own_cross/pallas_call | solution.py:378
  26.0 0.0 collective-permute-done.8.refs_3_
  26.0 0.0 collective-permute-done.6.refs_2_
  26.0 0.5 %pair_sums.2 = (f32[2,4,4,32,128]{4,3,2,1,0:T(8,128)S(1)}, f32[128,128]{1,0:T(8,128)S(1)}, f32[4,128]{1,0:T(4,128)S(1)}) custom-call(bf16[528,128]{1,0:T(8,128)(2,1)S(1)} %get-tuple-element.40.refs_0_, bf16[528,128]{1,0:T(8,128)(2,1)S(1)} %get-tuple-element.38.refs_1_, bf16[528,128]{1,0:T(8,128)(2,1)S(1)} %collective-permute-done.6.refs_2_, ...), custom_call_target="tpu_custom_call" | custom-call | tf_op jit(solution)/shard_map/pair_sums/pallas_call | solution.py:378
  26.5 0.0 collective-permute-done.9.refs_3_
  26.5 1.4 %pair_cross.3 = bf16[2,4,128,128]{3,2,1,0:T(8,128)(2,1)} custom-call(bf16[528,128]{1,0:T(8,128)(2,1)S(1)} %collective-permute-done.refs_2_.refs_0_, bf16[528,128]{1,0:T(8,128)(2,1)S(1)} %collective-permute-done.1.refs_3_.refs_1_, bf16[528,128]{1,0:T(8,128)(2,1)S(1)} %collective-permute-done.2.refs_2_, bf16[528,128]{1,0:T(8,128)(2,1)S(1)} %collective-permute-done.9.refs_3_, ...), custom_call_target="tpu_custom_call" | custom-call | tf_op jit(solution)/shard_map/pair_cross/pallas_call | solution.py:378
  27.9 0.0 collective-permute-done.4.refs_3_
  28.0 0.4 %collective-permute-done.3.refs_2_ = bf16[528,128]{1,0:T(8,128)(2,1)S(1)} collective-permute-done((bf16[528,128]{1,0:T(8,128)(2,1)S(1)}, bf16[528,128]{1,0:T(8,128)(2,1)S(1)}, u32[]{:S(2)}, u32[]{:S(2)}) %collective-permute-start.3) | collective-permute-done | bytes 135200 | tf_op jit(solution)/shard_map/ppermute | solution.py:457
  28.3 1.4 %pair_cross.2 = bf16[2,4,128,128]{3,2,1,0:T(8,128)(2,1)} custom-call(bf16[528,128]{1,0:T(8,128)(2,1)S(1)} %collective-permute-done.refs_2_.refs_0_, bf16[528,128]{1,0:T(8,128)(2,1)S(1)} %collective-permute-done.1.refs_3_.refs_1_, bf16[528,128]{1,0:T(8,128)(2,1)S(1)} %collective-permute-done.3.refs_2_, bf16[528,128]{1,0:T(8,128)(2,1)S(1)} %collective-permute-done.4.refs_3_, ...), custom_call_target="tpu_custom_call" | custom-call | tf_op jit(solution)/shard_map/pair_cross/pallas_call | solution.py:378
  (5 shorter events, 0.1 us)
Async XLA Ops:
  3.3 9.1 %collective-permute-start.7 = (bf16[528,128]{1,0:T(8,128)(2,1)S(1)}, bf16[528,128]{1,0:T(8,128)(2,1)S(1)}, u32[]{:S(2)}, u32[]{:S(2)}) collective-permute-start(bf16[528,128]{1,0:T(8,128)(2,1)S(1)} %get-tuple-element.38.refs_1_), channel_id=1, source_target_pairs={{8,0},{10,2},{12,4},{14,6},{16,8},{18,10},{20,12},{22,14},{24,16},... | collective-permute-start | bytes 405512 | tf_op jit(solution)/shard_map/ppermute | solution.py:398
  8.5 9.8 %collective-permute-start.5 = (bf16[528,128]{1,0:T(8,128)(2,1)S(1)}, bf16[528,128]{1,0:T(8,128)(2,1)S(1)}, u32[]{:S(2)}, u32[]{:S(2)}) collective-permute-start(bf16[528,128]{1,0:T(8,128)(2,1)S(1)} %get-tuple-element.40.refs_0_), channel_id=1, source_target_pairs={{8,0},{10,2},{12,4},{14,6},{16,8},{18,10},{20,12},{22,14},{24,16},... | collective-permute-start | bytes 405512 | tf_op jit(solution)/shard_map/ppermute | solution.py:398
  9.0 9.9 %collective-permute-start.1 = (bf16[528,128]{1,0:T(8,128)(2,1)S(1)}, bf16[528,128]{1,0:T(8,128)(2,1)S(1)}, u32[]{:S(2)}, u32[]{:S(2)}) collective-permute-start(bf16[528,128]{1,0:T(8,128)(2,1)S(1)} %get-tuple-element.37), channel_id=1, source_target_pairs={{1,0},{0,1},{3,2},{2,3},{5,4},{4,5},{7,6},{6,7},{9,8},{8,9},{11,10... | collective-permute-start | bytes 405512 | tf_op jit(solution)/shard_map/ppermute | solution.py:398
  10.4 6.2 %collective-permute-start = (bf16[528,128]{1,0:T(8,128)(2,1)S(1)}, bf16[528,128]{1,0:T(8,128)(2,1)S(1)}, u32[]{:S(2)}, u32[]{:S(2)}) collective-permute-start(bf16[528,128]{1,0:T(8,128)(2,1)S(1)} %get-tuple-element.39), channel_id=1, source_target_pairs={{1,0},{0,1},{3,2},{2,3},{5,4},{4,5},{7,6},{6,7},{9,8},{8,9},{11,10... | collective-permute-start | bytes 405512 | tf_op jit(solution)/shard_map/ppermute | solution.py:398
  12.4 13.6 %collective-permute-start.8 = (bf16[528,128]{1,0:T(8,128)(2,1)S(1)}, bf16[528,128]{1,0:T(8,128)(2,1)S(1)}, u32[]{:S(2)}, u32[]{:S(2)}) collective-permute-start(bf16[528,128]{1,0:T(8,128)(2,1)S(1)} %broadcast_select_fusion), channel_id=1, source_target_pairs={{0,4},{2,6},{4,0},{6,2},{8,12},{10,14},{12,8},{14,10},{16,20},{18,... | collective-permute-start | bytes 405512 | tf_op jit(solution)/shard_map/ppermute | solution.py:457
  16.6 6.4 %collective-permute-start.2 = (bf16[528,128]{1,0:T(8,128)(2,1)S(1)}, bf16[528,128]{1,0:T(8,128)(2,1)S(1)}, u32[]{:S(2)}, u32[]{:S(2)}) collective-permute-start(bf16[528,128]{1,0:T(8,128)(2,1)S(1)} %collective-permute-done.refs_2_.refs_0_), channel_id=1, source_target_pairs={{8,0},{10,2},{12,4},{14,6},{16,8},{18,10},{20,12},{22,14},{24,16},... | collective-permute-start | bytes 405512 | tf_op jit(solution)/shard_map/ppermute | solution.py:398
  18.3 7.7 %collective-permute-start.6 = (bf16[528,128]{1,0:T(8,128)(2,1)S(1)}, bf16[528,128]{1,0:T(8,128)(2,1)S(1)}, u32[]{:S(2)}, u32[]{:S(2)}) collective-permute-start(bf16[528,128]{1,0:T(8,128)(2,1)S(1)} %broadcast_select_fusion.1), channel_id=1, source_target_pairs={{0,4},{2,6},{4,0},{6,2},{8,12},{10,14},{12,8},{14,10},{16,20},{18,... | collective-permute-start | bytes 405512 | tf_op jit(solution)/shard_map/ppermute | solution.py:457
  18.9 7.6 %collective-permute-start.9 = (bf16[528,128]{1,0:T(8,128)(2,1)S(1)}, bf16[528,128]{1,0:T(8,128)(2,1)S(1)}, u32[]{:S(2)}, u32[]{:S(2)}) collective-permute-start(bf16[528,128]{1,0:T(8,128)(2,1)S(1)} %collective-permute-done.1.refs_3_.refs_1_), channel_id=1, source_target_pairs={{8,0},{10,2},{12,4},{14,6},{16,8},{18,10},{20,12},{22,14},{24,16},... | collective-permute-start | bytes 405512 | tf_op jit(solution)/shard_map/ppermute | solution.py:398
  20.1 7.9 %collective-permute-start.4 = (bf16[528,128]{1,0:T(8,128)(2,1)S(1)}, bf16[528,128]{1,0:T(8,128)(2,1)S(1)}, u32[]{:S(2)}, u32[]{:S(2)}) collective-permute-start(bf16[528,128]{1,0:T(8,128)(2,1)S(1)} %collective-permute-done.1.refs_3_.refs_1_), channel_id=1, source_target_pairs={{4,0},{6,2},{8,4},{10,6},{12,8},{14,10},{16,12},{18,14},{20,16},{2... | collective-permute-start | bytes 405512 | tf_op jit(solution)/shard_map/ppermute | solution.py:398
  23.1 1.0 %copy-start = (bf16[384,128]{1,0:T(8,128)(2,1)S(1)}, bf16[384,128]{1,0:T(8,128)(2,1)}, u32[]{:S(2)}) copy-start(bf16[384,128]{1,0:T(8,128)(2,1)} %constant.25.clone.refs_5_.refs_8_) | copy-start | bytes 294916
  23.1 1.0 %copy-start.1 = (f32[4096]{0:T(1024)S(1)}, f32[4096]{0:T(1024)}, u32[]{:S(2)}) copy-start(f32[4096]{0:T(1024)} %param.8) | copy-start | bytes 49156
  23.1 5.2 %collective-permute-start.3 = (bf16[528,128]{1,0:T(8,128)(2,1)S(1)}, bf16[528,128]{1,0:T(8,128)(2,1)S(1)}, u32[]{:S(2)}, u32[]{:S(2)}) collective-permute-start(bf16[528,128]{1,0:T(8,128)(2,1)S(1)} %broadcast_select_fusion.2), channel_id=1, source_target_pairs={{0,4},{2,6},{4,0},{6,2},{8,12},{10,14},{12,8},{14,10},{16,20},{18,... | collective-permute-start | bytes 405512 | tf_op jit(solution)/shard_map/ppermute | solution.py:457
where the time goes:
time: 29.9 us; the launch traced here: 29.8 us
  starting transfers between devices  15.8 us (53%)
  Pallas kernels  8.32 us (28%)
  waiting for transfers between devices  4.77 us (16%)
  between operations  0.77 us (3%)
    ppermute x7, starting transfers between devices, brought(): lax.ppermute(block, axis, [((i + distance) % count, i) for i in range(cou...  13.1 us
    pallas_call x5, Pallas kernels, cross(): pl.pallas_call(functools.partial(cross_kernel, stations=stations, windows...  5.7 us
    ppermute x7, waiting for transfers between devices, brought(): lax.ppermute(block, axis, [((i + distance) % count, i) for i in range(cou...  4.41 us
    ppermute x3, starting transfers between devices, program(): lax.ppermute(jnp.where(even, far[k][-1], held), 'sta', relay)  2.67 us
    pallas_call x1, Pallas kernels, transform(): pl.pallas_call(functools.partial(first_half_kernel, stations=stations, wi...  1.89 us
    pallas_call x1, Pallas kernels, transform(): pl.pallas_call(functools.partial(second_half_kernel, stations=per, window...  0.72 us
  transfers between devices with their start and end apart: 10, of which 4 were waited for; matrix products, arithmetic and copies ran while one was open for 0% of the time, Pallas kernels for 14%

commit v1 on v0

--- a/solution.py
+++ b/solution.py
@@ -14,10 +14,7 @@
 SMOOTH = 64
 epsilon = 1e-06
 
-C_HALVES = True
-X_HALVES = True
-O_HALVES = True
-DIAGONAL = ()
+CUT = 2
 DIRECT = ("1_1",)
 
 
@@ -42,8 +39,14 @@
     return jnp.asarray(np.abs(src - dst) <= SMOOTH, jnp.bfloat16)
 
 
-def parts_of(stations):
-    return 2 if stations % 2 == 0 else 1
+def pieces_of(stations):
+    return ((0, CUT), (CUT, stations - CUT)) if stations > CUT else ((0, stations),)
+
+
+def place_of(station, stations):
+    for h, (start, count) in enumerate(pieces_of(stations)):
+        if station < start + count:
+            return h, station - start
 
 
 def transformed(x, gate, held, outs, wide, edges, stations, windows, bands):
@@ -61,30 +64,31 @@
     lane = lax.broadcasted_iota(jnp.int32, (1, ROOT), 1)
     none = jnp.zeros((1, ROOT), jnp.float32)
     for s in range(stations):
-        wide[...] = x(s).astype(jnp.float32)
+        wide[s] = x(s).astype(jnp.float32)
         folded = jnp.concatenate(
             [
-                wide[pl.ds(w, ROOT, stride=windows), :].astype(jnp.bfloat16)
+                wide[s, pl.ds(w, ROOT, stride=windows), :].astype(jnp.bfloat16)
                 for w in range(windows)
             ],
             axis=1,
         )
         one = jnp.dot(first[...], folded, preferred_element_type=jnp.float32)
+        turned = []
         for w in range(windows):
             real = one[:ROOT, w * ROOT : (w + 1) * ROOT]
             imag = one[ROOT:, w * ROOT : (w + 1) * ROOT]
-            turned = jnp.concatenate(
-                [
-                    real * cosine[...] + imag * sine[...],
-                    imag * cosine[...] - real * sine[...],
-                ],
-                axis=1,
-            ).astype(jnp.bfloat16)
+            pair = [
+                real * cosine[...] + imag * sine[...],
+                imag * cosine[...] - real * sine[...],
+            ]
+            turned.append(jnp.concatenate(pair, axis=1).astype(jnp.bfloat16))
+        every = lax.dot_general(
+            second, jnp.concatenate(turned, axis=0), (((1,), (1,)), ((), ())),
+            preferred_element_type=jnp.float32,
+        )
+        for w in range(windows):
             at = s * windows + w
-            two = lax.dot_general(
-                second, turned, (((1,), (1,)), ((), ())),
-                preferred_element_type=jnp.float32,
-            ) * gate(at)
+            two = every[:, w * ROOT : (w + 1) * ROOT] * gate(at)
             for k in range(bands):
                 low, high = k * rows, (k + 1) * rows
                 for e in range(2):
@@ -100,8 +104,7 @@
 
 
 def first_half_kernel(given_flags, x_ref, given, given_turns, *refs, stations, windows, bands):
-    parts = parts_of(stations)
-    per = stations // parts
+    parts, per = len(pieces_of(stations)), pieces_of(stations)[0][1]
     outs, held, refs = refs[:bands], refs[bands : bands + 3], refs[bands + 3 :]
     if parts > 1:
         later, gates, *refs = refs
@@ -113,10 +116,10 @@
     arrivals = [
         pltpu.make_async_copy(x_ref.at[s], now.at[s], sems.at[2 + s]) for s in range(per)
     ]
-    for load in (load_flags, load_turns, load_first, *arrivals):
+    for load in (arrivals[0], load_first, load_turns, load_flags, *arrivals[1:]):
         load.start()
     if parts > 1:
-        rest = pltpu.make_async_copy(x_ref.at[pl.ds(per, per)], later, sems.at[2 + per])
+        rest = pltpu.make_async_copy(x_ref.at[pl.ds(per, stations - per)], later, sems.at[2 + per])
         rest.start()
 
     def flag(at):
@@ -124,7 +127,7 @@
 
     load_flags.wait()
     if parts > 1:
-        for at in range(per * windows):
+        for at in range((stations - per) * windows):
             gates[pl.ds(at, 1), :] = jnp.full((1, ROOT), flag(per * windows + at), jnp.float32)
     load_turns.wait()
     count = ROOT // 8
@@ -157,44 +160,48 @@
     packed = traces.reshape(stations, windows, ROOT, ROOT).transpose(0, 2, 1, 3)
     packed = packed.reshape(stations, ROOT * windows, ROOT)
     rows = ROOT // 2 // bands
-    parts = parts_of(stations)
-    per = stations // parts
-    height = 2 * per * windows * (rows + 1)
+    counts = [count for _, count in pieces_of(stations)]
     vmem = pl.BlockSpec(memory_space=pltpu.VMEM)
     hbm = pl.BlockSpec(memory_space=pl.ANY)
-    piece = pltpu.VMEM((height, ROOT), jnp.bfloat16)
     given = tables()
-    shape = (per, ROOT * windows, ROOT)
+
+    def outs_of(count):
+        return [pltpu.VMEM((2 * count * windows * (rows + 1), ROOT), jnp.bfloat16)] * bands
+
+    def block(count, dtype):
+        return pltpu.VMEM((count, ROOT * windows, ROOT), dtype)
+
+    def scratch_of(count):
+        edges = pltpu.VMEM((bands, 2 * count * windows, ROOT), jnp.float32)
+        return [block(count, jnp.float32), edges]
+
     turned = pltpu.VMEM((ROOT, ROOT), jnp.float32)
-    outs = [piece] * bands + [pltpu.VMEM(given[0].shape, jnp.bfloat16), turned, turned]
-    if parts > 1:
-        outs += [pltpu.VMEM(shape, jnp.bfloat16), pltpu.VMEM((per * windows, ROOT), jnp.float32)]
-    scratch = [
-        pltpu.VMEM((ROOT * windows, ROOT), jnp.float32),
-        pltpu.VMEM((bands, 2 * per * windows, ROOT), jnp.float32),
-    ]
+    outs = outs_of(counts[0]) + [pltpu.VMEM(given[0].shape, jnp.bfloat16), turned, turned]
+    for count in counts[1:]:
+        outs += [block(count, jnp.bfloat16), pltpu.VMEM((count * windows, ROOT), jnp.float32)]
     made = pl.pallas_call(
         functools.partial(first_half_kernel, stations=stations, windows=windows, bands=bands),
         out_shape=outs,
         in_specs=[hbm] * 4,
         out_specs=[vmem] * len(outs),
         scratch_shapes=[
-            pltpu.VMEM(shape, jnp.bfloat16), pltpu.VMEM(given[1].shape, jnp.float32), *scratch,
-            pltpu.SMEM(live_flag.shape, jnp.int32), pltpu.SemaphoreType.DMA((4 + per,)),
+            block(counts[0], jnp.bfloat16), pltpu.VMEM(given[1].shape, jnp.float32),
+            *scratch_of(counts[0]), pltpu.SMEM(live_flag.shape, jnp.int32),
+            pltpu.SemaphoreType.DMA((4 + counts[0],)),
         ],
         name="transform_first",
     )(live_flag, packed, *given)
     halves = [made[:bands]]
-    if parts > 1:
-        held, later, gates = made[bands : bands + 3], made[bands + 3], made[bands + 4]
+    for count in counts[1:]:
+        held, (later, gates) = made[bands : bands + 3], made[bands + 3 :]
         args = [pltpu.with_memory_space_constraint(v, pltpu.VMEM) for v in (later, gates, *held)]
         halves.append(
             pl.pallas_call(
-                functools.partial(second_half_kernel, stations=per, windows=windows, bands=bands),
-                out_shape=[piece] * bands,
+                functools.partial(second_half_kernel, stations=count, windows=windows, bands=bands),
+                out_shape=outs_of(count),
                 in_specs=[vmem] * len(args),
                 out_specs=[vmem] * bands,
-                scratch_shapes=scratch,
+                scratch_shapes=scratch_of(count),
                 name="transform_second",
             )(*args)
         )
@@ -215,31 +222,19 @@
     smooth = jnp.dot(low, window, preferred_element_type=jnp.float32)
     smooth = smooth + jnp.dot(high, window, preferred_element_type=jnp.float32)
     smooth = smooth * (1.0 / ((2 * SMOOTH + 1) * total))
-    return jnp.concatenate([gain] * stations, axis=0) / jnp.sqrt(smooth + epsilon)
-
-
-def cross_kernel(*refs, stations, windows, rows, merges, theirs, total, own, first, last):
+    return jnp.concatenate([gain] * stations, axis=0) * lax.rsqrt(smooth + epsilon)
+
+
+def cross_kernel(*refs, stations, windows, rows, chunks, total, own, first, last):
     refs = list(refs)
-    chunks, parts = len(merges), parts_of(stations)
-    per = stations // parts
+    parts = len(pieces_of(stations))
 
     def take(count):
         taken, refs[:] = refs[:count], refs[count:]
         return taken
 
-    def views(flags):
-        pieces = []
-        for merged in flags:
-            if merged:
-                height = 2 * per * windows * (rows + 1)
-                (ref,) = take(1)
-                pieces += [(ref, h * height) for h in range(parts)]
-            else:
-                pieces += [(ref, 0) for ref in take(parts)]
-        return pieces
-
-    left = views(merges)
-    right = left if own else views(theirs)
+    left = take(chunks * parts)
+    right = left if own else take(chunks * parts)
     if not first:
         sums, power_in, edge_in = take(3)
     if last:
@@ -251,19 +246,20 @@
     else:
         sums_out, power_out, edge_out = take(3)
 
-    body = 2 * per * windows * rows
     power, edge = [], []
     for s in range(stations):
+        h, place = place_of(s, stations)
+        body = 2 * pieces_of(stations)[h][1] * windows * rows
         cells = []
         lines = []
         for k in range(chunks):
-            chunk, base = right[k * parts + s // per]
+            chunk = right[k * parts + h]
             for w in range(windows):
-                at = 2 * (s % per * windows + w)
-                cell = chunk[pl.ds(base + at * rows, 2 * rows), :].astype(jnp.float32)
+                at = 2 * (place * windows + w)
+                cell = chunk[pl.ds(at * rows, 2 * rows), :].astype(jnp.float32)
                 cell = cell * cell
                 cells.append(cell[:rows] + cell[rows:])
-            line = chunk[pl.ds(base + body + 2 * (s % per) * windows, 2 * windows), :]
+            line = chunk[pl.ds(body + 2 * place * windows, 2 * windows), :]
             line = line.astype(jnp.float32)
             lines.append(jnp.sum(line * line, axis=0, keepdims=True))
         power.append(sum(cells[1:], cells[0]))
@@ -296,9 +292,9 @@
             real, imag = [None] * stations, [None] * stations
 
             def cell(pieces, k, s, w, e):
-                ref, base = pieces[k * parts + s // per]
-                at = base + ((s % per * windows + w) * 2 + e) * rows
-                return ref[pl.ds(pl.multiple_of(at + q, step), step), :]
+                h, place = place_of(s, stations)
+                at = ((place * windows + w) * 2 + e) * rows
+                return pieces[k * parts + h][pl.ds(pl.multiple_of(at + q, step), step), :]
 
             for k in range(chunks):
                 a = [cell(left, k, i, w, 0) for w in range(windows)]
@@ -342,10 +338,7 @@
 def cross(left, right, stations, windows, total, before=None, ends=None):
     own = right is None
     first, last = before is None, ends is not None
-    merges, theirs = (
-        tuple(len(chunk) == 1 and parts_of(stations) > 1 for chunk in side)
-        for side in (left, right or left)
-    )
+    chunks = len(left)
     height = sum(piece.shape[0] for piece in left[0])
     rows = height // (2 * stations * windows) - 1
     vmem = pl.BlockSpec(memory_space=pltpu.VMEM)
@@ -377,8 +370,8 @@
         scratch = []
     result = pl.pallas_call(
         functools.partial(
-            cross_kernel, stations=stations, windows=windows, rows=rows, merges=merges,
-            theirs=theirs,            total=total, own=own, first=first, last=last,
+            cross_kernel, stations=stations, windows=windows, rows=rows, chunks=chunks,
+            total=total, own=own, first=first, last=last,
         ),
         out_shape=outs,
         in_specs=[vmem] * len(args),
@@ -400,7 +393,7 @@
 
 def program(traces, live_flag, response):
     stations, windows, _ = traces.shape
-    bands, parts = lax.axis_size("band"), parts_of(stations)
+    bands, parts = lax.axis_size("band"), len(pieces_of(stations))
     band = lax.axis_index("band").astype(jnp.int32)
     blocks = lax.axis_size("sta")
     offset = blocks // 8
@@ -415,46 +408,17 @@
             return jnp.where(band == k, *pieces)
         return lax.select_n((band + k) % bands, *pieces) if bands > 1 else pieces[0]
 
-    def joined(k, hs):
-        return jnp.concatenate([sent(k, h) for h in hs], axis=0) if hs[1:] else sent(k, hs[0])
-
-    def groups(halves):
-        return [(h,) for h in range(parts)] if halves else [tuple(range(parts))]
-
-    def across(piece, distance, k):
-        if not k:
-            return brought(piece, "sta", distance)
-        route = [
-            ((s + distance) % blocks * bands + (b - k) % bands, s * bands + b)
-            for s in range(blocks)
-            for b in range(bands)
-        ]
-        return lax.ppermute(piece, ("sta", "band"), route)
-
     mine, far, near = ([[] for _ in range(bands)] for _ in range(3))
-    for k in range(bands):
-        for hs in groups(X_HALVES if k else C_HALVES):
-            piece = joined(k, hs)
-            mine[k].append(brought(piece, "band", -k) if k else piece)
-    for k in range(bands):
-        for at, hs in enumerate(groups(O_HALVES if k else C_HALVES)):
-            tag = f"{min(k, 1)}_{hs[0]}"
-            if k and tag not in DIAGONAL:
-                piece = mine[k][at]
-                far[k].append(brought(piece, "sta", 2 * offset))
-            else:
-                piece = joined(k, hs)
-                far[k].append(across(piece, 2 * offset, k))
-            if tag in DIRECT:
-                near[k].append(across(joined(k, hs), offset, k) if tag in DIAGONAL else brought(piece, "sta", offset))
-            else:
-                held = mine[k]
-                if len(held) > 1 or not O_HALVES or not k:
-                    held = held[at]
-                else:
-                    size = held[0].shape[0] // parts
-                    held = held[0][at * size : (at + 1) * size]
-                near[k].append(lax.ppermute(jnp.where(even, far[k][-1], held), "sta", relay))
+    order = [(k, h, f"{min(k, 1)}_{h}") for k in range(bands) for h in range(parts)]
+    for k, h, tag in order:
+        mine[k].append(brought(sent(k, h), "band", -k) if k else sent(k, h))
+    for k, h, tag in order:
+        far[k].append(brought(mine[k][h], "sta", 2 * offset))
+        if tag in DIRECT:
+            near[k].append(brought(mine[k][h], "sta", offset))
+        else:
+            held = jnp.where(even, far[k][h], mine[k][h])
+            near[k].append(lax.ppermute(held, "sta", relay))
     ends = [response.reshape(-1, ROOT), smoother()]
     own_cross, scale = cross(mine, None, stations, windows, total, ends=ends)
     ends.append(scale)

time: 29.9 us -> 29.9 us (level)
  no operation moved by 1% of the time
where the time goes in v1:
time: 29.9 us; the launch traced here: 29.7 us
  starting transfers between devices  15.8 us (53%)
  Pallas kernels  8.22 us (27%)
  waiting for transfers between devices  4.78 us (16%)
  between operations  0.77 us (3%)
    ppermute x7, starting transfers between devices, brought(): lax.ppermute(block, axis, [((i + distance) % count, i) for i in range(cou...  13.1 us
    pallas_call x5, Pallas kernels, cross(): pl.pallas_call(functools.partial(cross_kernel, stations=stations, windows...  5.66 us
    ppermute x7, waiting for transfers between devices, brought(): lax.ppermute(block, axis, [((i + distance) % count, i) for i in range(cou...  4.4 us
    ppermute x3, starting transfers between devices, program(): near[k].append(lax.ppermute(held, 'sta', relay))  2.71 us
    pallas_call x1, Pallas kernels, transform(): pl.pallas_call(functools.partial(first_half_kernel, stations=stations, wi...  1.84 us
    pallas_call x1, Pallas kernels, transform(): pl.pallas_call(functools.partial(second_half_kernel, stations=count, wind...  0.72 us
  transfers between devices with their start and end apart: 10, of which 4 were waited for; matrix products, arithmetic and copies ran while one was open for 0% of the time, Pallas kernels for 14%

profile of v1, /device:TPU:0, one launch (start us, length us, event | category | flops | bytes accessed | tf_op | source)
XLA Modules:
  0.0 29.7 jit_solution(12201677619677925876)
XLA Ops:
  0.6 1.8 %transform_first.1 = (bf16[528,128]{1,0:T(8,128)(2,1)S(1)}, bf16[528,128]{1,0:T(8,128)(2,1)S(1)}, bf16[256,128]{1,0:T(8,128)(2,1)S(1)}, f32[128,128]{1,0:T(8,128...) custom-call(s32[4,8]{1,0:T(4,128)} %given_flags.1, ...), custom_call_target="tpu_custom_call" | custom-call | tf_op jit(solution)/shard_map/transform_first/pallas_call | solution.py:182
  2.5 0.7 %transform_second.1 = (bf16[528,128]{1,0:T(8,128)(2,1)S(1)}, bf16[528,128]{1,0:T(8,128)(2,1)S(1)}) custom-call(bf16[2,512,128]{2,1,0:T(8,128)(2,1)S(1)} %get-tuple-element.22.x_ref, f32[8,128]{1,0:T(8,128)S(1)} %get-tuple-element.23.gates, bf16[256,128]{1,0:T(8,128)(2,1)S(1)} %get-tuple-element.24.refs_0_, f32[128,128]{1,0:T(8,128)S(1)} %get-tuple-element.25.refs_1_, ...), custom_call_target="tpu_custom_call" | custom-call | tf_op jit(solution)/shard_map/transform_second/pallas_call | solution.py:199
  3.2 5.1 %collective-permute-start.7 = (bf16[528,128]{1,0:T(8,128)(2,1)S(1)}, bf16[528,128]{1,0:T(8,128)(2,1)S(1)}, u32[]{:S(2)}, u32[]{:S(2)}) collective-permute-start(bf16[528,128]{1,0:T(8,128)(2,1)S(1)} %get-tuple-element.38.refs_1_), channel_id=1, source_target_pairs={{8,0},{10,2},{12,4},{14,6},{16,8},{18,10},{20,12},{22,14},{24,16},... | collective-permute-start | bytes 405512 | tf_op jit(solution)/shard_map/ppermute | solution.py:391
  8.4 0.5 %collective-permute-start.5 = (bf16[528,128]{1,0:T(8,128)(2,1)S(1)}, bf16[528,128]{1,0:T(8,128)(2,1)S(1)}, u32[]{:S(2)}, u32[]{:S(2)}) collective-permute-start(bf16[528,128]{1,0:T(8,128)(2,1)S(1)} %get-tuple-element.40.refs_0_), channel_id=1, source_target_pairs={{8,0},{10,2},{12,4},{14,6},{16,8},{18,10},{20,12},{22,14},{24,16},... | collective-permute-start | bytes 405512 | tf_op jit(solution)/shard_map/ppermute | solution.py:391
  8.9 1.5 %collective-permute-start.1 = (bf16[528,128]{1,0:T(8,128)(2,1)S(1)}, bf16[528,128]{1,0:T(8,128)(2,1)S(1)}, u32[]{:S(2)}, u32[]{:S(2)}) collective-permute-start(bf16[528,128]{1,0:T(8,128)(2,1)S(1)} %get-tuple-element.37), channel_id=1, source_target_pairs={{1,0},{0,1},{3,2},{2,3},{5,4},{4,5},{7,6},{6,7},{9,8},{8,9},{11,10... | collective-permute-start | bytes 405512 | tf_op jit(solution)/shard_map/ppermute | solution.py:391
  10.4 0.5 %collective-permute-start = (bf16[528,128]{1,0:T(8,128)(2,1)S(1)}, bf16[528,128]{1,0:T(8,128)(2,1)S(1)}, u32[]{:S(2)}, u32[]{:S(2)}) collective-permute-start(bf16[528,128]{1,0:T(8,128)(2,1)S(1)} %get-tuple-element.39), channel_id=1, source_target_pairs={{1,0},{0,1},{3,2},{2,3},{5,4},{4,5},{7,6},{6,7},{9,8},{8,9},{11,10... | collective-permute-start | bytes 405512 | tf_op jit(solution)/shard_map/ppermute | solution.py:391
  10.9 1.4 %collective-permute-done.7.refs_3_ = bf16[528,128]{1,0:T(8,128)(2,1)S(1)} collective-permute-done((bf16[528,128]{1,0:T(8,128)(2,1)S(1)}, bf16[528,128]{1,0:T(8,128)(2,1)S(1)}, u32[]{:S(2)}, u32[]{:S(2)}) %collective-permute-start.7) | collective-permute-done | bytes 135200 | tf_op jit(solution)/shard_map/ppermute | solution.py:391
  12.4 1.6 %collective-permute-start.8 = (bf16[528,128]{1,0:T(8,128)(2,1)S(1)}, bf16[528,128]{1,0:T(8,128)(2,1)S(1)}, u32[]{:S(2)}, u32[]{:S(2)}) collective-permute-start(bf16[528,128]{1,0:T(8,128)(2,1)S(1)} %broadcast_select_fusion), channel_id=1, source_target_pairs={{0,4},{2,6},{4,0},{6,2},{8,12},{10,14},{12,8},{14,10},{16,20},{18,... | collective-permute-start | bytes 405512 | tf_op jit(solution)/shard_map/ppermute | solution.py:421
  14.0 2.6 %collective-permute-done.refs_2_.refs_0_ = bf16[528,128]{1,0:T(8,128)(2,1)S(1)} collective-permute-done((bf16[528,128]{1,0:T(8,128)(2,1)S(1)}, bf16[528,128]{1,0:T(8,128)(2,1)S(1)}, u32[]{:S(2)}, u32[]{:S(2)}) %collective-permute-start) | collective-permute-done | bytes 135200 | tf_op jit(solution)/shard_map/ppermute | solution.py:391
  16.6 1.7 %collective-permute-start.2 = (bf16[528,128]{1,0:T(8,128)(2,1)S(1)}, bf16[528,128]{1,0:T(8,128)(2,1)S(1)}, u32[]{:S(2)}, u32[]{:S(2)}) collective-permute-start(bf16[528,128]{1,0:T(8,128)(2,1)S(1)} %collective-permute-done.refs_2_.refs_0_), channel_id=1, source_target_pairs={{8,0},{10,2},{12,4},{14,6},{16,8},{18,10},{20,12},{22,14},{24,16},... | collective-permute-start | bytes 405512 | tf_op jit(solution)/shard_map/ppermute | solution.py:391
  18.2 0.0 collective-permute-done.5.refs_2_
  18.3 0.6 %collective-permute-start.6 = (bf16[528,128]{1,0:T(8,128)(2,1)S(1)}, bf16[528,128]{1,0:T(8,128)(2,1)S(1)}, u32[]{:S(2)}, u32[]{:S(2)}) collective-permute-start(bf16[528,128]{1,0:T(8,128)(2,1)S(1)} %broadcast_select_fusion.1), channel_id=1, source_target_pairs={{0,4},{2,6},{4,0},{6,2},{8,12},{10,14},{12,8},{14,10},{16,20},{18,... | collective-permute-start | bytes 405512 | tf_op jit(solution)/shard_map/ppermute | solution.py:421
  18.8 0.0 collective-permute-done.1.refs_3_.refs_1_
  18.8 1.2 %collective-permute-start.9 = (bf16[528,128]{1,0:T(8,128)(2,1)S(1)}, bf16[528,128]{1,0:T(8,128)(2,1)S(1)}, u32[]{:S(2)}, u32[]{:S(2)}) collective-permute-start(bf16[528,128]{1,0:T(8,128)(2,1)S(1)} %collective-permute-done.1.refs_3_.refs_1_), channel_id=1, source_target_pairs={{8,0},{10,2},{12,4},{14,6},{16,8},{18,10},{20,12},{22,14},{24,16},... | collective-permute-start | bytes 405512 | tf_op jit(solution)/shard_map/ppermute | solution.py:391
  20.0 2.6 %collective-permute-start.4 = (bf16[528,128]{1,0:T(8,128)(2,1)S(1)}, bf16[528,128]{1,0:T(8,128)(2,1)S(1)}, u32[]{:S(2)}, u32[]{:S(2)}) collective-permute-start(bf16[528,128]{1,0:T(8,128)(2,1)S(1)} %collective-permute-done.1.refs_3_.refs_1_), channel_id=1, source_target_pairs={{4,0},{6,2},{8,4},{10,6},{12,8},{14,10},{16,12},{18,14},{20,16},{2... | collective-permute-start | bytes 405512 | tf_op jit(solution)/shard_map/ppermute | solution.py:391
  22.6 0.3 %collective-permute-done.2.refs_2_ = bf16[528,128]{1,0:T(8,128)(2,1)S(1)} collective-permute-done((bf16[528,128]{1,0:T(8,128)(2,1)S(1)}, bf16[528,128]{1,0:T(8,128)(2,1)S(1)}, u32[]{:S(2)}, u32[]{:S(2)}) %collective-permute-start.2) | collective-permute-done | bytes 135200 | tf_op jit(solution)/shard_map/ppermute | solution.py:391
  23.0 0.0 copy-start
  23.0 0.0 copy-start.1
  23.0 0.6 %collective-permute-start.3 = (bf16[528,128]{1,0:T(8,128)(2,1)S(1)}, bf16[528,128]{1,0:T(8,128)(2,1)S(1)}, u32[]{:S(2)}, u32[]{:S(2)}) collective-permute-start(bf16[528,128]{1,0:T(8,128)(2,1)S(1)} %broadcast_select_fusion.2), channel_id=1, source_target_pairs={{0,4},{2,6},{4,0},{6,2},{8,12},{10,14},{12,8},{14,10},{16,20},{18,... | collective-permute-start | bytes 405512 | tf_op jit(solution)/shard_map/ppermute | solution.py:421
  23.6 0.5 %pair_sums.3 = (f32[2,4,4,32,128]{4,3,2,1,0:T(8,128)S(1)}, f32[128,128]{1,0:T(8,128)S(1)}, f32[4,128]{1,0:T(4,128)S(1)}) custom-call(bf16[528,128]{1,0:T(8,128)(2,1)S(1)} %get-tuple-element.40.refs_0_, bf16[528,128]{1,0:T(8,128)(2,1)S(1)} %get-tuple-element.38.refs_1_, bf16[528,128]{1,0:T(8,128)(2,1)S(1)} %collective-permute-done.5.refs_2_, ...), custom_call_target="tpu_custom_call" | custom-call | tf_op jit(solution)/shard_map/pair_sums/pallas_call | solution.py:371
  24.0 0.0 copy-done
  24.1 0.0 copy-done.1
  24.1 1.9 %own_cross.1 = (bf16[2,4,128,128]{3,2,1,0:T(8,128)(2,1)}, f32[128,128]{1,0:T(8,128)S(1)}) custom-call(bf16[528,128]{1,0:T(8,128)(2,1)S(1)} %get-tuple-element.40.refs_0_, bf16[528,128]{1,0:T(8,128)(2,1)S(1)} %get-tuple-element.38.refs_1_, bf16[528,128]{1,0:T(8,128)(2,1)S(1)} %collective-permute-done.refs_2_.refs_0_, ...), custom_call_target="tpu_custom_call" | custom-call | tf_op jit(solution)/shard_map/own_cross/pallas_call | solution.py:371
  25.9 0.0 collective-permute-done.8.refs_3_
  26.0 0.0 collective-permute-done.6.refs_2_
  26.0 0.5 %pair_sums.2 = (f32[2,4,4,32,128]{4,3,2,1,0:T(8,128)S(1)}, f32[128,128]{1,0:T(8,128)S(1)}, f32[4,128]{1,0:T(4,128)S(1)}) custom-call(bf16[528,128]{1,0:T(8,128)(2,1)S(1)} %get-tuple-element.40.refs_0_, bf16[528,128]{1,0:T(8,128)(2,1)S(1)} %get-tuple-element.38.refs_1_, bf16[528,128]{1,0:T(8,128)(2,1)S(1)} %collective-permute-done.6.refs_2_, ...), custom_call_target="tpu_custom_call" | custom-call | tf_op jit(solution)/shard_map/pair_sums/pallas_call | solution.py:371
  26.4 0.0 collective-permute-done.9.refs_3_
  26.4 1.4 %pair_cross.3 = bf16[2,4,128,128]{3,2,1,0:T(8,128)(2,1)} custom-call(bf16[528,128]{1,0:T(8,128)(2,1)S(1)} %collective-permute-done.refs_2_.refs_0_, bf16[528,128]{1,0:T(8,128)(2,1)S(1)} %collective-permute-done.1.refs_3_.refs_1_, bf16[528,128]{1,0:T(8,128)(2,1)S(1)} %collective-permute-done.2.refs_2_, bf16[528,128]{1,0:T(8,128)(2,1)S(1)} %collective-permute-done.9.refs_3_, ...), custom_call_target="tpu_custom_call" | custom-call | tf_op jit(solution)/shard_map/pair_cross/pallas_call | solution.py:371
  27.9 0.0 collective-permute-done.4.refs_3_
  27.9 0.4 %collective-permute-done.3.refs_2_ = bf16[528,128]{1,0:T(8,128)(2,1)S(1)} collective-permute-done((bf16[528,128]{1,0:T(8,128)(2,1)S(1)}, bf16[528,128]{1,0:T(8,128)(2,1)S(1)}, u32[]{:S(2)}, u32[]{:S(2)}) %collective-permute-start.3) | collective-permute-done | bytes 135200 | tf_op jit(solution)/shard_map/ppermute | solution.py:421
  28.3 1.4 %pair_cross.2 = bf16[2,4,128,128]{3,2,1,0:T(8,128)(2,1)} custom-call(bf16[528,128]{1,0:T(8,128)(2,1)S(1)} %collective-permute-done.refs_2_.refs_0_, bf16[528,128]{1,0:T(8,128)(2,1)S(1)} %collective-permute-done.1.refs_3_.refs_1_, bf16[528,128]{1,0:T(8,128)(2,1)S(1)} %collective-permute-done.3.refs_2_, bf16[528,128]{1,0:T(8,128)(2,1)S(1)} %collective-permute-done.4.refs_3_, ...), custom_call_target="tpu_custom_call" | custom-call | tf_op jit(solution)/shard_map/pair_cross/pallas_call | solution.py:371
  (5 shorter events, 0.1 us)
Async XLA Ops:
  3.2 9.1 %collective-permute-start.7 = (bf16[528,128]{1,0:T(8,128)(2,1)S(1)}, bf16[528,128]{1,0:T(8,128)(2,1)S(1)}, u32[]{:S(2)}, u32[]{:S(2)}) collective-permute-start(bf16[528,128]{1,0:T(8,128)(2,1)S(1)} %get-tuple-element.38.refs_1_), channel_id=1, source_target_pairs={{8,0},{10,2},{12,4},{14,6},{16,8},{18,10},{20,12},{22,14},{24,16},... | collective-permute-start | bytes 405512 | tf_op jit(solution)/shard_map/ppermute | solution.py:391
  8.4 9.8 %collective-permute-start.5 = (bf16[528,128]{1,0:T(8,128)(2,1)S(1)}, bf16[528,128]{1,0:T(8,128)(2,1)S(1)}, u32[]{:S(2)}, u32[]{:S(2)}) collective-permute-start(bf16[528,128]{1,0:T(8,128)(2,1)S(1)} %get-tuple-element.40.refs_0_), channel_id=1, source_target_pairs={{8,0},{10,2},{12,4},{14,6},{16,8},{18,10},{20,12},{22,14},{24,16},... | collective-permute-start | bytes 405512 | tf_op jit(solution)/shard_map/ppermute | solution.py:391
  8.9 9.9 %collective-permute-start.1 = (bf16[528,128]{1,0:T(8,128)(2,1)S(1)}, bf16[528,128]{1,0:T(8,128)(2,1)S(1)}, u32[]{:S(2)}, u32[]{:S(2)}) collective-permute-start(bf16[528,128]{1,0:T(8,128)(2,1)S(1)} %get-tuple-element.37), channel_id=1, source_target_pairs={{1,0},{0,1},{3,2},{2,3},{5,4},{4,5},{7,6},{6,7},{9,8},{8,9},{11,10... | collective-permute-start | bytes 405512 | tf_op jit(solution)/shard_map/ppermute | solution.py:391
  10.4 6.2 %collective-permute-start = (bf16[528,128]{1,0:T(8,128)(2,1)S(1)}, bf16[528,128]{1,0:T(8,128)(2,1)S(1)}, u32[]{:S(2)}, u32[]{:S(2)}) collective-permute-start(bf16[528,128]{1,0:T(8,128)(2,1)S(1)} %get-tuple-element.39), channel_id=1, source_target_pairs={{1,0},{0,1},{3,2},{2,3},{5,4},{4,5},{7,6},{6,7},{9,8},{8,9},{11,10... | collective-permute-start | bytes 405512 | tf_op jit(solution)/shard_map/ppermute | solution.py:391
  12.4 13.6 %collective-permute-start.8 = (bf16[528,128]{1,0:T(8,128)(2,1)S(1)}, bf16[528,128]{1,0:T(8,128)(2,1)S(1)}, u32[]{:S(2)}, u32[]{:S(2)}) collective-permute-start(bf16[528,128]{1,0:T(8,128)(2,1)S(1)} %broadcast_select_fusion), channel_id=1, source_target_pairs={{0,4},{2,6},{4,0},{6,2},{8,12},{10,14},{12,8},{14,10},{16,20},{18,... | collective-permute-start | bytes 405512 | tf_op jit(solution)/shard_map/ppermute | solution.py:421
  16.6 6.4 %collective-permute-start.2 = (bf16[528,128]{1,0:T(8,128)(2,1)S(1)}, bf16[528,128]{1,0:T(8,128)(2,1)S(1)}, u32[]{:S(2)}, u32[]{:S(2)}) collective-permute-start(bf16[528,128]{1,0:T(8,128)(2,1)S(1)} %collective-permute-done.refs_2_.refs_0_), channel_id=1, source_target_pairs={{8,0},{10,2},{12,4},{14,6},{16,8},{18,10},{20,12},{22,14},{24,16},... | collective-permute-start | bytes 405512 | tf_op jit(solution)/shard_map/ppermute | solution.py:391
  18.3 7.7 %collective-permute-start.6 = (bf16[528,128]{1,0:T(8,128)(2,1)S(1)}, bf16[528,128]{1,0:T(8,128)(2,1)S(1)}, u32[]{:S(2)}, u32[]{:S(2)}) collective-permute-start(bf16[528,128]{1,0:T(8,128)(2,1)S(1)} %broadcast_select_fusion.1), channel_id=1, source_target_pairs={{0,4},{2,6},{4,0},{6,2},{8,12},{10,14},{12,8},{14,10},{16,20},{18,... | collective-permute-start | bytes 405512 | tf_op jit(solution)/shard_map/ppermute | solution.py:421
  18.8 7.6 %collective-permute-start.9 = (bf16[528,128]{1,0:T(8,128)(2,1)S(1)}, bf16[528,128]{1,0:T(8,128)(2,1)S(1)}, u32[]{:S(2)}, u32[]{:S(2)}) collective-permute-start(bf16[528,128]{1,0:T(8,128)(2,1)S(1)} %collective-permute-done.1.refs_3_.refs_1_), channel_id=1, source_target_pairs={{8,0},{10,2},{12,4},{14,6},{16,8},{18,10},{20,12},{22,14},{24,16},... | collective-permute-start | bytes 405512 | tf_op jit(solution)/shard_map/ppermute | solution.py:391
  20.0 7.9 %collective-permute-start.4 = (bf16[528,128]{1,0:T(8,128)(2,1)S(1)}, bf16[528,128]{1,0:T(8,128)(2,1)S(1)}, u32[]{:S(2)}, u32[]{:S(2)}) collective-permute-start(bf16[528,128]{1,0:T(8,128)(2,1)S(1)} %collective-permute-done.1.refs_3_.refs_1_), channel_id=1, source_target_pairs={{4,0},{6,2},{8,4},{10,6},{12,8},{14,10},{16,12},{18,14},{20,16},{2... | collective-permute-start | bytes 405512 | tf_op jit(solution)/shard_map/ppermute | solution.py:391
  23.0 1.1 %copy-start = (bf16[384,128]{1,0:T(8,128)(2,1)S(1)}, bf16[384,128]{1,0:T(8,128)(2,1)}, u32[]{:S(2)}) copy-start(bf16[384,128]{1,0:T(8,128)(2,1)} %constant.25.clone.refs_5_.refs_8_) | copy-start | bytes 294916
  23.0 1.1 %copy-start.1 = (f32[4096]{0:T(1024)S(1)}, f32[4096]{0:T(1024)}, u32[]{:S(2)}) copy-start(f32[4096]{0:T(1024)} %param.8) | copy-start | bytes 49156
  23.0 5.2 %collective-permute-start.3 = (bf16[528,128]{1,0:T(8,128)(2,1)S(1)}, bf16[528,128]{1,0:T(8,128)(2,1)S(1)}, u32[]{:S(2)}, u32[]{:S(2)}) collective-permute-start(bf16[528,128]{1,0:T(8,128)(2,1)S(1)} %broadcast_select_fusion.2), channel_id=1, source_target_pairs={{0,4},{2,6},{4,0},{6,2},{8,12},{10,14},{12,8},{14,10},{16,20},{18,... | collective-permute-start | bytes 405512 | tf_op jit(solution)/shard_map/ppermute | solution.py:421

commit v2 on v1

--- a/solution.py
+++ b/solution.py
@@ -242,6 +242,7 @@
         scale_left = None if own else take(1)[0]
         (out,) = take(1)
         scale_right, board, ready, sems = take(4)
+        kept = take(1)[0] if own else None
         scale_left = scale_right if own else scale_left
     else:
         sums_out, power_out, edge_out = take(3)
@@ -299,7 +300,7 @@
             for k in range(chunks):
                 a = [cell(left, k, i, w, 0) for w in range(windows)]
                 b = [cell(left, k, i, w, 1) for w in range(windows)]
-                for j in range(stations):
+                for j in range(i if own else 0, stations):
                     c = [cell(right, k, j, w, 0) for w in range(windows)]
                     d = [cell(right, k, j, w, 1) for w in range(windows)]
                     re = tree([a[w] * c[w] + b[w] * d[w] for w in range(windows)])
@@ -311,9 +312,15 @@
                 here = here * (1.0 / total)
             for j in range(stations):
                 to = pl.ds(q, step)
-                if not first:
+                if own and j < i:
+                    if not last:
+                        continue
+                    real[j], imag[j] = kept[0, j, i, to, :], -kept[1, j, i, to, :]
+                elif not first:
                     real[j] = real[j] + sums[0, i, j, to, :]
                     imag[j] = imag[j] + sums[1, i, j, to, :]
+                if own and last and j > i:
+                    kept[0, i, j, to, :], kept[1, i, j, to, :] = real[j], imag[j]
                 if last:
                     there = scale_right[pl.ds(pl.multiple_of(j * rows + q, step), step), :]
                     to = pl.ds(q * stations + j, step, stride=stations)
@@ -324,7 +331,7 @@
                     sums_out[1, i, j, to, :] = imag[j]
             return carry
 
-        lax.fori_loop(0, steps, turn, 0)
+        lax.fori_loop(0, steps, turn, 0, unroll=True)
         if last:
             ready[:, i] = board[...].astype(jnp.bfloat16)
             for e in range(2):
@@ -358,6 +365,7 @@
         if own:
             outs.append(pltpu.VMEM(scales, jnp.float32))
             out_specs.append(vmem)
+            scratch.append(pltpu.VMEM((2, stations, stations, rows, ROOT), jnp.float32))
         else:
             scratch.insert(0, pltpu.VMEM(scales, jnp.float32))
     else:
@@ -377,7 +385,6 @@
         in_specs=[vmem] * len(args),
         out_specs=out_specs,
         scratch_shapes=scratch,
-        name="own_cross" if own else "pair_cross" if last else "pair_sums",
     )(*args)
     if not last:
         return result
@@ -420,17 +427,20 @@
             held = jnp.where(even, far[k][h], mine[k][h])
             near[k].append(lax.ppermute(held, "sta", relay))
     ends = [response.reshape(-1, ROOT), smoother()]
-    own_cross, scale = cross(mine, None, stations, windows, total, ends=ends)
+
+    def summed(theirs):
+        return cross(mine[:1], theirs, stations, windows, total) if bands > 1 else None
+
+    def ended(theirs, before):
+        rest = slice(1 if before else 0, None)
+        theirs = theirs and theirs[rest]
+        return cross(mine[rest], theirs, stations, windows, total, before=before, ends=ends)
+
+    sums = summed(None)
+    own_cross, scale = ended(None, sums)
     ends.append(scale)
-
-    def pair(theirs):
-        if bands == 1:
-            return cross(mine, theirs, stations, windows, total, ends=ends)
-        sums = cross(mine[:1], theirs[:1], stations, windows, total)
-        return cross(mine[1:], theirs[1:], stations, windows, total, before=sums, ends=ends)
-
-    far_cross = pair(far)
-    near_cross = pair(near)
+    far_cross = ended(far, summed(far[:1]))
+    near_cross = ended(near, summed(near[:1]))
     return own_cross, near_cross, far_cross
 
 

time: 29.9 us -> 29.8 us (level)
  Pallas kernels: 8.22 us -> 7.29 us
  local copies, waits for them, and re-layouts: 0.01 us -> 0.55 us
  waiting for transfers between devices: 4.78 us -> 5.09 us
    pallas_call x5 -> x6, Pallas kernels: 5.66 us -> 4.73 us  [cross(): pl.pallas_call(functools.partial(cross_kernel, stations=stations, windows...]
    unnamed x4, local copies, waits for them, and re-layouts: 0.01 us -> 0.55 us
    ppermute x3, waiting for transfers between devices: 0.37 us -> 0.68 us  [program(): near[k].append(lax.ppermute(held, 'sta', relay))]
  transfers between devices with their start and end apart: 10 -> 10, of which waited for: 4 -> 4; matrix products, arithmetic and copies ran while one was open for 0% -> 0% of each run, Pallas kernels for 14% -> 11%
where the time goes in v2:
time: 29.8 us; the launch traced here: 29.6 us
  starting transfers between devices  15.8 us (53%)
  Pallas kernels  7.29 us (24%)
  waiting for transfers between devices  5.09 us (17%)
  between operations  0.75 us (3%)
  local copies, waits for them, and re-layouts  0.55 us (2%)
    ppermute x7, starting transfers between devices, brought(): lax.ppermute(block, axis, [((i + distance) % count, i) for i in range(cou...  13.1 us
    pallas_call x6, Pallas kernels, cross(): pl.pallas_call(functools.partial(cross_kernel, stations=stations, windows...  4.73 us
    ppermute x7, waiting for transfers between devices, brought(): lax.ppermute(block, axis, [((i + distance) % count, i) for i in range(cou...  4.4 us
    ppermute x3, starting transfers between devices, program(): near[k].append(lax.ppermute(held, 'sta', relay))  2.71 us
    pallas_call x1, Pallas kernels, transform(): pl.pallas_call(functools.partial(first_half_kernel, stations=stations, wi...  1.84 us
    pallas_call x1, Pallas kernels, transform(): pl.pallas_call(functools.partial(second_half_kernel, stations=count, wind...  0.72 us
    ppermute x3, waiting for transfers between devices, program(): near[k].append(lax.ppermute(held, 'sta', relay))  0.68 us
  transfers between devices with their start and end apart: 10, of which 4 were waited for; matrix products, arithmetic and copies ran while one was open for 0% of the time, Pallas kernels for 11%

profile of v2, /device:TPU:0, one launch (start us, length us, event | category | flops | bytes accessed | tf_op | source)
XLA Modules:
  0.0 29.6 jit_solution(13729311963595166708)
XLA Ops:
  0.6 1.8 %transform_first.1 = (bf16[528,128]{1,0:T(8,128)(2,1)S(1)}, bf16[528,128]{1,0:T(8,128)(2,1)S(1)}, bf16[256,128]{1,0:T(8,128)(2,1)S(1)}, f32[128,128]{1,0:T(8,128...) custom-call(s32[4,8]{1,0:T(4,128)} %given_flags.1, ...), custom_call_target="tpu_custom_call" | custom-call | tf_op jit(solution)/shard_map/transform_first/pallas_call | solution.py:182
  2.5 0.7 %transform_second.1 = (bf16[528,128]{1,0:T(8,128)(2,1)S(1)}, bf16[528,128]{1,0:T(8,128)(2,1)S(1)}) custom-call(bf16[2,512,128]{2,1,0:T(8,128)(2,1)S(1)} %get-tuple-element.25.x_ref, f32[8,128]{1,0:T(8,128)S(1)} %get-tuple-element.26.gates, bf16[256,128]{1,0:T(8,128)(2,1)S(1)} %get-tuple-element.27.refs_0_, f32[128,128]{1,0:T(8,128)S(1)} %get-tuple-element.28.refs_1_, ...), custom_call_target="tpu_custom_call" | custom-call | tf_op jit(solution)/shard_map/transform_second/pallas_call | solution.py:199
  3.2 5.1 %collective-permute-start.7 = (bf16[528,128]{1,0:T(8,128)(2,1)S(1)}, bf16[528,128]{1,0:T(8,128)(2,1)S(1)}, u32[]{:S(2)}, u32[]{:S(2)}) collective-permute-start(bf16[528,128]{1,0:T(8,128)(2,1)S(1)} %get-tuple-element.43.refs_1_), channel_id=1, source_target_pairs={{8,0},{10,2},{12,4},{14,6},{16,8},{18,10},{20,12},{22,14},{24,16},... | collective-permute-start | bytes 405512 | tf_op jit(solution)/shard_map/ppermute | solution.py:398
  8.4 0.5 %collective-permute-start.5 = (bf16[528,128]{1,0:T(8,128)(2,1)S(1)}, bf16[528,128]{1,0:T(8,128)(2,1)S(1)}, u32[]{:S(2)}, u32[]{:S(2)}) collective-permute-start(bf16[528,128]{1,0:T(8,128)(2,1)S(1)} %get-tuple-element.45.refs_0_), channel_id=1, source_target_pairs={{8,0},{10,2},{12,4},{14,6},{16,8},{18,10},{20,12},{22,14},{24,16},... | collective-permute-start | bytes 405512 | tf_op jit(solution)/shard_map/ppermute | solution.py:398
  8.9 1.5 %collective-permute-start.1 = (bf16[528,128]{1,0:T(8,128)(2,1)S(1)}, bf16[528,128]{1,0:T(8,128)(2,1)S(1)}, u32[]{:S(2)}, u32[]{:S(2)}) collective-permute-start(bf16[528,128]{1,0:T(8,128)(2,1)S(1)} %get-tuple-element.44), channel_id=1, source_target_pairs={{1,0},{0,1},{3,2},{2,3},{5,4},{4,5},{7,6},{6,7},{9,8},{8,9},{11,10... | collective-permute-start | bytes 405512 | tf_op jit(solution)/shard_map/ppermute | solution.py:398
  10.4 0.5 %collective-permute-start = (bf16[528,128]{1,0:T(8,128)(2,1)S(1)}, bf16[528,128]{1,0:T(8,128)(2,1)S(1)}, u32[]{:S(2)}, u32[]{:S(2)}) collective-permute-start(bf16[528,128]{1,0:T(8,128)(2,1)S(1)} %get-tuple-element.46), channel_id=1, source_target_pairs={{1,0},{0,1},{3,2},{2,3},{5,4},{4,5},{7,6},{6,7},{9,8},{8,9},{11,10... | collective-permute-start | bytes 405512 | tf_op jit(solution)/shard_map/ppermute | solution.py:398
  10.9 1.4 %collective-permute-done.7.refs_3_ = bf16[528,128]{1,0:T(8,128)(2,1)S(1)} collective-permute-done((bf16[528,128]{1,0:T(8,128)(2,1)S(1)}, bf16[528,128]{1,0:T(8,128)(2,1)S(1)}, u32[]{:S(2)}, u32[]{:S(2)}) %collective-permute-start.7) | collective-permute-done | bytes 135200 | tf_op jit(solution)/shard_map/ppermute | solution.py:398
  12.4 1.6 %collective-permute-start.8 = (bf16[528,128]{1,0:T(8,128)(2,1)S(1)}, bf16[528,128]{1,0:T(8,128)(2,1)S(1)}, u32[]{:S(2)}, u32[]{:S(2)}) collective-permute-start(bf16[528,128]{1,0:T(8,128)(2,1)S(1)} %broadcast_select_fusion), channel_id=1, source_target_pairs={{0,4},{2,6},{4,0},{6,2},{8,12},{10,14},{12,8},{14,10},{16,20},{18,... | collective-permute-start | bytes 405512 | tf_op jit(solution)/shard_map/ppermute | solution.py:428
  14.0 2.6 %collective-permute-done.refs_0_ = bf16[528,128]{1,0:T(8,128)(2,1)S(1)} collective-permute-done((bf16[528,128]{1,0:T(8,128)(2,1)S(1)}, bf16[528,128]{1,0:T(8,128)(2,1)S(1)}, u32[]{:S(2)}, u32[]{:S(2)}) %collective-permute-start) | collective-permute-done | bytes 135200 | tf_op jit(solution)/shard_map/ppermute | solution.py:398
  16.6 1.7 %collective-permute-start.2 = (bf16[528,128]{1,0:T(8,128)(2,1)S(1)}, bf16[528,128]{1,0:T(8,128)(2,1)S(1)}, u32[]{:S(2)}, u32[]{:S(2)}) collective-permute-start(bf16[528,128]{1,0:T(8,128)(2,1)S(1)} %collective-permute-done.refs_0_), channel_id=1, source_target_pairs={{8,0},{10,2},{12,4},{14,6},{16,8},{18,10},{20,12},{22,14},{24,16},... | collective-permute-start | bytes 405512 | tf_op jit(solution)/shard_map/ppermute | solution.py:398
  18.2 0.0 collective-permute-done.5.refs_2_
  18.3 0.6 %collective-permute-start.6 = (bf16[528,128]{1,0:T(8,128)(2,1)S(1)}, bf16[528,128]{1,0:T(8,128)(2,1)S(1)}, u32[]{:S(2)}, u32[]{:S(2)}) collective-permute-start(bf16[528,128]{1,0:T(8,128)(2,1)S(1)} %broadcast_select_fusion.1), channel_id=1, source_target_pairs={{0,4},{2,6},{4,0},{6,2},{8,12},{10,14},{12,8},{14,10},{16,20},{18,... | collective-permute-start | bytes 405512 | tf_op jit(solution)/shard_map/ppermute | solution.py:428
  18.8 0.0 collective-permute-done.1.refs_1_
  18.8 1.2 %collective-permute-start.9 = (bf16[528,128]{1,0:T(8,128)(2,1)S(1)}, bf16[528,128]{1,0:T(8,128)(2,1)S(1)}, u32[]{:S(2)}, u32[]{:S(2)}) collective-permute-start(bf16[528,128]{1,0:T(8,128)(2,1)S(1)} %collective-permute-done.1.refs_1_), channel_id=1, source_target_pairs={{8,0},{10,2},{12,4},{14,6},{16,8},{18,10},{20,12},{22,14},{24,16},... | collective-permute-start | bytes 405512 | tf_op jit(solution)/shard_map/ppermute | solution.py:398
  20.0 2.6 %collective-permute-start.4 = (bf16[528,128]{1,0:T(8,128)(2,1)S(1)}, bf16[528,128]{1,0:T(8,128)(2,1)S(1)}, u32[]{:S(2)}, u32[]{:S(2)}) collective-permute-start(bf16[528,128]{1,0:T(8,128)(2,1)S(1)} %collective-permute-done.1.refs_1_), channel_id=1, source_target_pairs={{4,0},{6,2},{8,4},{10,6},{12,8},{14,10},{16,12},{18,14},{20,16},{2... | collective-permute-start | bytes 405512 | tf_op jit(solution)/shard_map/ppermute | solution.py:398
  22.6 0.3 %collective-permute-done.2.refs_2_ = bf16[528,128]{1,0:T(8,128)(2,1)S(1)} collective-permute-done((bf16[528,128]{1,0:T(8,128)(2,1)S(1)}, bf16[528,128]{1,0:T(8,128)(2,1)S(1)}, u32[]{:S(2)}, u32[]{:S(2)}) %collective-permute-start.2) | collective-permute-done | bytes 135200 | tf_op jit(solution)/shard_map/ppermute | solution.py:398
  23.0 0.6 %collective-permute-start.3 = (bf16[528,128]{1,0:T(8,128)(2,1)S(1)}, bf16[528,128]{1,0:T(8,128)(2,1)S(1)}, u32[]{:S(2)}, u32[]{:S(2)}) collective-permute-start(bf16[528,128]{1,0:T(8,128)(2,1)S(1)} %broadcast_select_fusion.2), channel_id=1, source_target_pairs={{0,4},{2,6},{4,0},{6,2},{8,12},{10,14},{12,8},{14,10},{16,20},{18,... | collective-permute-start | bytes 405512 | tf_op jit(solution)/shard_map/ppermute | solution.py:428
  23.6 0.2 shard_map.85
  23.8 0.0 copy-start
  23.8 0.0 copy-start.1
  23.8 0.3 %shard_map.89 = (f32[2,4,4,32,128]{4,3,2,1,0:T(8,128)S(1)}, f32[128,128]{1,0:T(8,128)S(1)}, f32[4,128]{1,0:T(4,128)S(1)}) custom-call(bf16[528,128]{1,0:T(8,128)(2,1)S(1)} %get-tuple-element.45.refs_0_, bf16[528,128]{1,0:T(8,128)(2,1)S(1)} %get-tuple-element.43.refs_1_, bf16[528,128]{1,0:T(8,128)(2,1)S(1)} %collective-permute-done.5.refs_2_, ...), custom_call_target="tpu_custom_call" | custom-call | tf_op jit(solution)/shard_map/pallas_call | solution.py:379
  24.1 0.5 %copy-done = bf16[384,128]{1,0:T(8,128)(2,1)S(1)} copy-done((bf16[384,128]{1,0:T(8,128)(2,1)S(1)}, bf16[384,128]{1,0:T(8,128)(2,1)}, u32[]{:S(2)}) %copy-start) | copy-done | bytes 98328
  24.7 0.0 copy-done.1
  24.7 1.2 %shard_map.86 = (bf16[2,4,128,128]{3,2,1,0:T(8,128)(2,1)}, f32[128,128]{1,0:T(8,128)S(1)}) custom-call(bf16[528,128]{1,0:T(8,128)(2,1)S(1)} %collective-permute-done.refs_0_, bf16[528,128]{1,0:T(8,128)(2,1)S(1)} %collective-permute-done.1.refs_1_, f32[2,4,4,32,128]{4,3,2,1,0:T(8,128)S(1)} %get-tuple-element.32.refs_2_, ...), custom_call_target="tpu_custom_call" | custom-call | tf_op jit(solution)/shard_map/pallas_call | solution.py:379
  25.9 0.0 collective-permute-done.8.refs_3_
  25.9 0.0 collective-permute-done.6.refs_2_
  25.9 0.3 %shard_map.87 = (f32[2,4,4,32,128]{4,3,2,1,0:T(8,128)S(1)}, f32[128,128]{1,0:T(8,128)S(1)}, f32[4,128]{1,0:T(4,128)S(1)}) custom-call(bf16[528,128]{1,0:T(8,128)(2,1)S(1)} %get-tuple-element.45.refs_0_, bf16[528,128]{1,0:T(8,128)(2,1)S(1)} %get-tuple-element.43.refs_1_, bf16[528,128]{1,0:T(8,128)(2,1)S(1)} %collective-permute-done.6.refs_2_, ...), custom_call_target="tpu_custom_call" | custom-call | tf_op jit(solution)/shard_map/pallas_call | solution.py:379
  26.2 0.0 collective-permute-done.9.refs_3_
  26.2 1.3 %shard_map.90 = bf16[2,4,128,128]{3,2,1,0:T(8,128)(2,1)} custom-call(bf16[528,128]{1,0:T(8,128)(2,1)S(1)} %collective-permute-done.refs_0_, bf16[528,128]{1,0:T(8,128)(2,1)S(1)} %collective-permute-done.1.refs_1_, bf16[528,128]{1,0:T(8,128)(2,1)S(1)} %collective-permute-done.2.refs_2_, bf16[528,128]{1,0:T(8,128)(2,1)S(1)} %collective-permute-done.9.refs_3_, ...), custom_call_target="tpu_custom_call" | custom-call | tf_op jit(solution)/shard_map/pallas_call | solution.py:379
  27.6 0.0 collective-permute-done.4.refs_3_
  27.6 0.7 %collective-permute-done.3.refs_2_ = bf16[528,128]{1,0:T(8,128)(2,1)S(1)} collective-permute-done((bf16[528,128]{1,0:T(8,128)(2,1)S(1)}, bf16[528,128]{1,0:T(8,128)(2,1)S(1)}, u32[]{:S(2)}, u32[]{:S(2)}) %collective-permute-start.3) | collective-permute-done | bytes 135200 | tf_op jit(solution)/shard_map/ppermute | solution.py:428
  28.3 1.3 %shard_map.88 = bf16[2,4,128,128]{3,2,1,0:T(8,128)(2,1)} custom-call(bf16[528,128]{1,0:T(8,128)(2,1)S(1)} %collective-permute-done.refs_0_, bf16[528,128]{1,0:T(8,128)(2,1)S(1)} %collective-permute-done.1.refs_1_, bf16[528,128]{1,0:T(8,128)(2,1)S(1)} %collective-permute-done.3.refs_2_, bf16[528,128]{1,0:T(8,128)(2,1)S(1)} %collective-permute-done.4.refs_3_, ...), custom_call_target="tpu_custom_call" | custom-call | tf_op jit(solution)/shard_map/pallas_call | solution.py:379
  (5 shorter events, 0.1 us)
Async XLA Ops:
  3.2 9.1 %collective-permute-start.7 = (bf16[528,128]{1,0:T(8,128)(2,1)S(1)}, bf16[528,128]{1,0:T(8,128)(2,1)S(1)}, u32[]{:S(2)}, u32[]{:S(2)}) collective-permute-start(bf16[528,128]{1,0:T(8,128)(2,1)S(1)} %get-tuple-element.43.refs_1_), channel_id=1, source_target_pairs={{8,0},{10,2},{12,4},{14,6},{16,8},{18,10},{20,12},{22,14},{24,16},... | collective-permute-start | bytes 405512 | tf_op jit(solution)/shard_map/ppermute | solution.py:398
  8.4 9.8 %collective-permute-start.5 = (bf16[528,128]{1,0:T(8,128)(2,1)S(1)}, bf16[528,128]{1,0:T(8,128)(2,1)S(1)}, u32[]{:S(2)}, u32[]{:S(2)}) collective-permute-start(bf16[528,128]{1,0:T(8,128)(2,1)S(1)} %get-tuple-element.45.refs_0_), channel_id=1, source_target_pairs={{8,0},{10,2},{12,4},{14,6},{16,8},{18,10},{20,12},{22,14},{24,16},... | collective-permute-start | bytes 405512 | tf_op jit(solution)/shard_map/ppermute | solution.py:398
  8.9 9.9 %collective-permute-start.1 = (bf16[528,128]{1,0:T(8,128)(2,1)S(1)}, bf16[528,128]{1,0:T(8,128)(2,1)S(1)}, u32[]{:S(2)}, u32[]{:S(2)}) collective-permute-start(bf16[528,128]{1,0:T(8,128)(2,1)S(1)} %get-tuple-element.44), channel_id=1, source_target_pairs={{1,0},{0,1},{3,2},{2,3},{5,4},{4,5},{7,6},{6,7},{9,8},{8,9},{11,10... | collective-permute-start | bytes 405512 | tf_op jit(solution)/shard_map/ppermute | solution.py:398
  10.4 6.2 %collective-permute-start = (bf16[528,128]{1,0:T(8,128)(2,1)S(1)}, bf16[528,128]{1,0:T(8,128)(2,1)S(1)}, u32[]{:S(2)}, u32[]{:S(2)}) collective-permute-start(bf16[528,128]{1,0:T(8,128)(2,1)S(1)} %get-tuple-element.46), channel_id=1, source_target_pairs={{1,0},{0,1},{3,2},{2,3},{5,4},{4,5},{7,6},{6,7},{9,8},{8,9},{11,10... | collective-permute-start | bytes 405512 | tf_op jit(solution)/shard_map/ppermute | solution.py:398
  12.4 13.5 %collective-permute-start.8 = (bf16[528,128]{1,0:T(8,128)(2,1)S(1)}, bf16[528,128]{1,0:T(8,128)(2,1)S(1)}, u32[]{:S(2)}, u32[]{:S(2)}) collective-permute-start(bf16[528,128]{1,0:T(8,128)(2,1)S(1)} %broadcast_select_fusion), channel_id=1, source_target_pairs={{0,4},{2,6},{4,0},{6,2},{8,12},{10,14},{12,8},{14,10},{16,20},{18,... | collective-permute-start | bytes 405512 | tf_op jit(solution)/shard_map/ppermute | solution.py:428
  16.6 6.4 %collective-permute-start.2 = (bf16[528,128]{1,0:T(8,128)(2,1)S(1)}, bf16[528,128]{1,0:T(8,128)(2,1)S(1)}, u32[]{:S(2)}, u32[]{:S(2)}) collective-permute-start(bf16[528,128]{1,0:T(8,128)(2,1)S(1)} %collective-permute-done.refs_0_), channel_id=1, source_target_pairs={{8,0},{10,2},{12,4},{14,6},{16,8},{18,10},{20,12},{22,14},{24,16},... | collective-permute-start | bytes 405512 | tf_op jit(solution)/shard_map/ppermute | solution.py:398
  18.3 7.6 %collective-permute-start.6 = (bf16[528,128]{1,0:T(8,128)(2,1)S(1)}, bf16[528,128]{1,0:T(8,128)(2,1)S(1)}, u32[]{:S(2)}, u32[]{:S(2)}) collective-permute-start(bf16[528,128]{1,0:T(8,128)(2,1)S(1)} %broadcast_select_fusion.1), channel_id=1, source_target_pairs={{0,4},{2,6},{4,0},{6,2},{8,12},{10,14},{12,8},{14,10},{16,20},{18,... | collective-permute-start | bytes 405512 | tf_op jit(solution)/shard_map/ppermute | solution.py:428
  18.8 7.4 %collective-permute-start.9 = (bf16[528,128]{1,0:T(8,128)(2,1)S(1)}, bf16[528,128]{1,0:T(8,128)(2,1)S(1)}, u32[]{:S(2)}, u32[]{:S(2)}) collective-permute-start(bf16[528,128]{1,0:T(8,128)(2,1)S(1)} %collective-permute-done.1.refs_1_), channel_id=1, source_target_pairs={{8,0},{10,2},{12,4},{14,6},{16,8},{18,10},{20,12},{22,14},{24,16},... | collective-permute-start | bytes 405512 | tf_op jit(solution)/shard_map/ppermute | solution.py:398
  20.0 7.6 %collective-permute-start.4 = (bf16[528,128]{1,0:T(8,128)(2,1)S(1)}, bf16[528,128]{1,0:T(8,128)(2,1)S(1)}, u32[]{:S(2)}, u32[]{:S(2)}) collective-permute-start(bf16[528,128]{1,0:T(8,128)(2,1)S(1)} %collective-permute-done.1.refs_1_), channel_id=1, source_target_pairs={{4,0},{6,2},{8,4},{10,6},{12,8},{14,10},{16,12},{18,14},{20,16},{2... | collective-permute-start | bytes 405512 | tf_op jit(solution)/shard_map/ppermute | solution.py:398
  23.0 5.3 %collective-permute-start.3 = (bf16[528,128]{1,0:T(8,128)(2,1)S(1)}, bf16[528,128]{1,0:T(8,128)(2,1)S(1)}, u32[]{:S(2)}, u32[]{:S(2)}) collective-permute-start(bf16[528,128]{1,0:T(8,128)(2,1)S(1)} %broadcast_select_fusion.2), channel_id=1, source_target_pairs={{0,4},{2,6},{4,0},{6,2},{8,12},{10,14},{12,8},{14,10},{16,20},{18,... | collective-permute-start | bytes 405512 | tf_op jit(solution)/shard_map/ppermute | solution.py:428
  23.8 0.9 %copy-start = (bf16[384,128]{1,0:T(8,128)(2,1)S(1)}, bf16[384,128]{1,0:T(8,128)(2,1)}, u32[]{:S(2)}) copy-start(bf16[384,128]{1,0:T(8,128)(2,1)} %constant.25.clone.refs_6_.refs_8_) | copy-start | bytes 294916
  23.8 0.9 %copy-start.1 = (f32[4096]{0:T(1024)S(1)}, f32[4096]{0:T(1024)}, u32[]{:S(2)}) copy-start(f32[4096]{0:T(1024)} %param.8) | copy-start | bytes 49156
